TPU v7x, 32 devices: a whole 2x2x4 slice. The times are simulated.
32 devices in a mesh: panel: 16 (over z, y, x), obs: 2 (over core).
Axes of the slice: x: 2, y: 2, z: 4, core: 2. Of those that a mesh axis runs over, the one named last changes fastest.
Arguments:
- donor: bfloat16 [128, 125, 4, 256], P('panel', None, None, 'obs'), may hold values from -6 to 6
- donor_elem: int32 [2048], P('obs'), may hold values from 0 to 255, as said below
- local_coords: float32 [3, 2048], P(None, 'obs'), may hold values from -1 to 1
- owner: int32 [2048], replicated, may hold values from 0 to 15, as said below
- weights: bfloat16 [256, 4, 4, 2048], P('obs', None, None, 'panel'), may hold values from -0.03125 to 0.03125
- offsets: int32 [2, 16], P('obs', 'panel'), may hold values from 0 to 64
Outputs:
- pressure: float32 [128, 256], P('panel', 'obs')
Inputs may be any that keep to these rules, and one draw needn't show every extreme that they name: `donor_elem`: point i lies in a donor element of the i // 1024-th block of 128 elements. Every owner owns exactly 128 points. Within each of the 2 aligned blocks of 1024 points an owner appears either 80 times or 128 / 2 - 128 / 8 times, and exactly one block holds 80 of its points.
All inputs are finite; a program needn't handle non-finite values.
Results may differ from a plain program's by a relative error of at most 0.0029.
Values may be sent and summed in bfloat16 or wider, within the bound.
No kernel may reach another device: no remote copies, remote signals or barrier semaphores. Data moves between devices by JAX's collectives and lax.ppermute only.
A program may use at most 64 MiB of HBM per device.

v0:
```python
import jax
import jax.numpy as jnp
from jax import lax
from jax.sharding import PartitionSpec as P

BAND = 4
OBLK = 128
PTILE = 128


NODE_SPOTS = (-1.0, -0.5, 0.0, 0.5, 1.0)


def lagrange_table(coords):
    factors = []
    for direction in range(3):
        coord_row = coords[direction]
        columns = []
        for node_one in range(5):
            weighting = jnp.ones_like(coord_row)
            for node_two in range(5):
                if node_two != node_one:
                    weighting = weighting * (
                        (coord_row - NODE_SPOTS[node_two])
                        / (NODE_SPOTS[node_one] - NODE_SPOTS[node_two])
                    )
            columns.append(weighting)
        factors.append(jnp.stack(columns))
    node_table = (
        factors[0][:, None, None, :] * factors[1][None, :, None, :] * factors[2][None, None, :, :]
    )
    return node_table.reshape(125, coords.shape[1])


def body(donor, donor_elem, local_coords, owner, weights, offsets):
    share_index = lax.axis_index("obs")
    elem_local = donor_elem - share_index * donor.shape[3]
    node_table = lagrange_table(local_coords)

    def one_time(moment):
        values = jnp.take(moment, elem_local, axis=2)
        return jnp.sum(node_table[:, None, :] * values, axis=0).astype(jnp.bfloat16)

    local_sources = lax.map(one_time, donor)
    order = jnp.argsort(owner, stable=True)
    everything = lax.all_gather(local_sources, "obs", axis=2, tiled=True)
    outgoing = jnp.take(everything, order, axis=2)
    sources = lax.all_to_all(outgoing, "panel", split_axis=2, concat_axis=0, tiled=True)
    total_time = sources.shape[0]
    front = total_time // 2 + BAND - 1
    padded = jnp.pad(sources, ((front, 0), (0, 0), (0, 0)))
    delay_steps = offsets[0, 0]
    base = 0 + front - delay_steps
    stacked = jnp.stack(
        [lax.dynamic_slice_in_dim(padded, base - delay, total_time, 0) for delay in range(BAND)],
        axis=1,
    )
    stacked = stacked.reshape(total_time, BAND * padded.shape[1] * PTILE)
    weight_tile = weights
    weight_tile = weight_tile.reshape(OBLK, stacked.shape[1])
    running = lax.dot_general(
        stacked, weight_tile, (((1,), (1,)), ((), ())), preferred_element_type=jnp.float32
    )
    pressure = lax.psum_scatter(running, "panel", scatter_dimension=0, tiled=True)
    return pressure


def solution(mesh):
    return jax.shard_map(
        body,
        mesh=mesh,
        in_specs=(
            P("panel", None, None, "obs"),
            P("obs"),
            P(None, "obs"),
            P(),
            P("obs", None, None, "panel"),
            P("obs", "panel"),
        ),
        out_specs=P("panel", "obs"),
        check_vma=False,
    )
```

profile of v0, /device:TPU:0, one launch (start us, length us, event | category | flops | bytes accessed | tf_op | source)
XLA Modules:
  0.0 335.1 jit_solution(8465294150786984933)
XLA Ops:
  6.5 5.8 %sort.17 = (s32[2048]{0:T(1024)}, s32[2048]{0:T(1024)S(1)}) sort(s32[2048]{0:T(1024)} %param.11, s32[2048]{0:T(1024)S(1)} %iota.4), dimensions={0}, to_apply=%region_0.1 | sort | flops 22528 | bytes 32768 | tf_op jit(solution)/shard_map/jit(argsort)/sort | solution.py:45
  12.4 1.0 multiply_multiply_fusion.10
  13.3 0.7 broadcast_subtract_fusion
  14.2 160.1 %while.11 = (s32[]{:T(128)}, bf16[8,4,1024]{2,0,1:T(8,128)(2,1)S(1)}, s32[1024]{0:T(1024)S(1)}, bf16[8,125,4,128]{3,2,1,0:T(4,128)(2,1)}, f32[5,1024]{1,0:T(8,12...) while((s32[]{:T(128)}, bf16[8,4,1024]{2,0,1:T(8,128)(2,1)S(1)}, s32[1024]{0:T(1024)S(1)}, ...), condition=%wide.region_3.4_spmd.clone, body=%wide.region_1.0_spmd.clone.sunk | while | flops 2182146 | bytes 6846565 | solution.py:44
  14.2 1.0 constant_dynamic-slice_fusion.3
  15.2 0.2 copy.37
  15.5 0.2 copy.38
  15.8 3.6 %gather_fusion = bf16[1024,125,4]{1,2,0:T(4,128)(2,1)S(1)} fusion(bf16[125,4,128]{0,1,2:T(4,128)(2,1)S(1)} %bitcast.52, s32[1024]{0:T(1024)S(1)} %broadcast_clamp_fusion.2), kind=kCustom, calls=%fused_computation.clone.clone.1 | custom fusion | bytes 2052096 | tf_op jit(solution)/shard_map/while/body/eval_jaxpr/jit(_take)/gather | solution.py:41
  19.3 14.5 %fusion.19 = bf16[4,1024]{0,1:T(8,128)(2,1)S(1)} fusion(bf16[1024,125,4]{1,2,0:T(4,128)(2,1)S(1)} %gather_fusion, f32[125,1024]{0,1:T(8,128)S(1)} %copy.38, pred[1024]{0:T(1024)(128)(4,1)S(1)} %compare_and_fusion.3), kind=kLoop, calls=%fused_computation.4.clone.1 | loop fusion | flops 2043904 | bytes 1545216 | tf_op jit(solution)/shard_map/while/body/eval_jaxpr/reduce_sum | solution.py:42
  33.8 0.2 copy.39
  34.2 1.0 constant_dynamic-slice_fusion.3
  35.2 0.2 copy.37
  35.5 0.2 copy.38
  35.8 3.6 %gather_fusion = bf16[1024,125,4]{1,2,0:T(4,128)(2,1)S(1)} fusion(bf16[125,4,128]{0,1,2:T(4,128)(2,1)S(1)} %bitcast.52, s32[1024]{0:T(1024)S(1)} %broadcast_clamp_fusion.2), kind=kCustom, calls=%fused_computation.clone.clone.1 | custom fusion | bytes 2052096 | tf_op jit(solution)/shard_map/while/body/eval_jaxpr/jit(_take)/gather | solution.py:41
  39.4 14.5 %fusion.19 = bf16[4,1024]{0,1:T(8,128)(2,1)S(1)} fusion(bf16[1024,125,4]{1,2,0:T(4,128)(2,1)S(1)} %gather_fusion, f32[125,1024]{0,1:T(8,128)S(1)} %copy.38, pred[1024]{0:T(1024)(128)(4,1)S(1)} %compare_and_fusion.3), kind=kLoop, calls=%fused_computation.4.clone.1 | loop fusion | flops 2043904 | bytes 1545216 | tf_op jit(solution)/shard_map/while/body/eval_jaxpr/reduce_sum | solution.py:42
  53.9 0.2 copy.39
  54.2 1.0 constant_dynamic-slice_fusion.3
  55.2 0.2 copy.37
  55.6 0.2 copy.38
  55.8 3.6 %gather_fusion = bf16[1024,125,4]{1,2,0:T(4,128)(2,1)S(1)} fusion(bf16[125,4,128]{0,1,2:T(4,128)(2,1)S(1)} %bitcast.52, s32[1024]{0:T(1024)S(1)} %broadcast_clamp_fusion.2), kind=kCustom, calls=%fused_computation.clone.clone.1 | custom fusion | bytes 2052096 | tf_op jit(solution)/shard_map/while/body/eval_jaxpr/jit(_take)/gather | solution.py:41
  59.4 14.5 %fusion.19 = bf16[4,1024]{0,1:T(8,128)(2,1)S(1)} fusion(bf16[1024,125,4]{1,2,0:T(4,128)(2,1)S(1)} %gather_fusion, f32[125,1024]{0,1:T(8,128)S(1)} %copy.38, pred[1024]{0:T(1024)(128)(4,1)S(1)} %compare_and_fusion.3), kind=kLoop, calls=%fused_computation.4.clone.1 | loop fusion | flops 2043904 | bytes 1545216 | tf_op jit(solution)/shard_map/while/body/eval_jaxpr/reduce_sum | solution.py:42
  73.9 0.2 copy.39
  74.2 1.0 constant_dynamic-slice_fusion.3
  75.2 0.2 copy.37
  75.6 0.2 copy.38
  75.8 3.6 %gather_fusion = bf16[1024,125,4]{1,2,0:T(4,128)(2,1)S(1)} fusion(bf16[125,4,128]{0,1,2:T(4,128)(2,1)S(1)} %bitcast.52, s32[1024]{0:T(1024)S(1)} %broadcast_clamp_fusion.2), kind=kCustom, calls=%fused_computation.clone.clone.1 | custom fusion | bytes 2052096 | tf_op jit(solution)/shard_map/while/body/eval_jaxpr/jit(_take)/gather | solution.py:41
  79.4 14.5 %fusion.19 = bf16[4,1024]{0,1:T(8,128)(2,1)S(1)} fusion(bf16[1024,125,4]{1,2,0:T(4,128)(2,1)S(1)} %gather_fusion, f32[125,1024]{0,1:T(8,128)S(1)} %copy.38, pred[1024]{0:T(1024)(128)(4,1)S(1)} %compare_and_fusion.3), kind=kLoop, calls=%fused_computation.4.clone.1 | loop fusion | flops 2043904 | bytes 1545216 | tf_op jit(solution)/shard_map/while/body/eval_jaxpr/reduce_sum | solution.py:42
  93.9 0.2 copy.39
  94.3 1.0 constant_dynamic-slice_fusion.3
  95.2 0.2 copy.37
  95.6 0.2 copy.38
  95.8 3.6 %gather_fusion = bf16[1024,125,4]{1,2,0:T(4,128)(2,1)S(1)} fusion(bf16[125,4,128]{0,1,2:T(4,128)(2,1)S(1)} %bitcast.52, s32[1024]{0:T(1024)S(1)} %broadcast_clamp_fusion.2), kind=kCustom, calls=%fused_computation.clone.clone.1 | custom fusion | bytes 2052096 | tf_op jit(solution)/shard_map/while/body/eval_jaxpr/jit(_take)/gather | solution.py:41
  99.4 14.5 %fusion.19 = bf16[4,1024]{0,1:T(8,128)(2,1)S(1)} fusion(bf16[1024,125,4]{1,2,0:T(4,128)(2,1)S(1)} %gather_fusion, f32[125,1024]{0,1:T(8,128)S(1)} %copy.38, pred[1024]{0:T(1024)(128)(4,1)S(1)} %compare_and_fusion.3), kind=kLoop, calls=%fused_computation.4.clone.1 | loop fusion | flops 2043904 | bytes 1545216 | tf_op jit(solution)/shard_map/while/body/eval_jaxpr/reduce_sum | solution.py:42
  113.9 0.2 copy.39
  114.3 1.0 constant_dynamic-slice_fusion.3
  115.2 0.2 copy.37
  115.6 0.2 copy.38
  115.8 3.6 %gather_fusion = bf16[1024,125,4]{1,2,0:T(4,128)(2,1)S(1)} fusion(bf16[125,4,128]{0,1,2:T(4,128)(2,1)S(1)} %bitcast.52, s32[1024]{0:T(1024)S(1)} %broadcast_clamp_fusion.2), kind=kCustom, calls=%fused_computation.clone.clone.1 | custom fusion | bytes 2052096 | tf_op jit(solution)/shard_map/while/body/eval_jaxpr/jit(_take)/gather | solution.py:41
  119.4 14.5 %fusion.19 = bf16[4,1024]{0,1:T(8,128)(2,1)S(1)} fusion(bf16[1024,125,4]{1,2,0:T(4,128)(2,1)S(1)} %gather_fusion, f32[125,1024]{0,1:T(8,128)S(1)} %copy.38, pred[1024]{0:T(1024)(128)(4,1)S(1)} %compare_and_fusion.3), kind=kLoop, calls=%fused_computation.4.clone.1 | loop fusion | flops 2043904 | bytes 1545216 | tf_op jit(solution)/shard_map/while/body/eval_jaxpr/reduce_sum | solution.py:42
  133.9 0.2 copy.39
  134.3 1.0 constant_dynamic-slice_fusion.3
  135.6 0.2 copy.38
  135.8 3.6 %gather_fusion = bf16[1024,125,4]{1,2,0:T(4,128)(2,1)S(1)} fusion(bf16[125,4,128]{0,1,2:T(4,128)(2,1)S(1)} %bitcast.52, s32[1024]{0:T(1024)S(1)} %broadcast_clamp_fusion.2), kind=kCustom, calls=%fused_computation.clone.clone.1 | custom fusion | bytes 2052096 | tf_op jit(solution)/shard_map/while/body/eval_jaxpr/jit(_take)/gather | solution.py:41
  139.4 14.5 %fusion.19 = bf16[4,1024]{0,1:T(8,128)(2,1)S(1)} fusion(bf16[1024,125,4]{1,2,0:T(4,128)(2,1)S(1)} %gather_fusion, f32[125,1024]{0,1:T(8,128)S(1)} %copy.38, pred[1024]{0:T(1024)(128)(4,1)S(1)} %compare_and_fusion.3), kind=kLoop, calls=%fused_computation.4.clone.1 | loop fusion | flops 2043904 | bytes 1545216 | tf_op jit(solution)/shard_map/while/body/eval_jaxpr/reduce_sum | solution.py:42
  153.9 0.2 copy.39
  154.3 1.0 constant_dynamic-slice_fusion.3
  155.6 0.2 copy.38
  155.8 3.6 %gather_fusion = bf16[1024,125,4]{1,2,0:T(4,128)(2,1)S(1)} fusion(bf16[125,4,128]{0,1,2:T(4,128)(2,1)S(1)} %bitcast.52, s32[1024]{0:T(1024)S(1)} %broadcast_clamp_fusion.2), kind=kCustom, calls=%fused_computation.clone.clone.1 | custom fusion | bytes 2052096 | tf_op jit(solution)/shard_map/while/body/eval_jaxpr/jit(_take)/gather | solution.py:41
  159.4 14.5 %fusion.19 = bf16[4,1024]{0,1:T(8,128)(2,1)S(1)} fusion(bf16[1024,125,4]{1,2,0:T(4,128)(2,1)S(1)} %gather_fusion, f32[125,1024]{0,1:T(8,128)S(1)} %copy.38, pred[1024]{0:T(1024)(128)(4,1)S(1)} %compare_and_fusion.3), kind=kLoop, calls=%fused_computation.4.clone.1 | loop fusion | flops 2043904 | bytes 1545216 | tf_op jit(solution)/shard_map/while/body/eval_jaxpr/reduce_sum | solution.py:42
  173.9 0.2 copy.39
  174.2 2.0 all_gather.3
  176.3 1.3 copy.24
  177.6 14.5 %gather_fusion.1 = bf16[2048,8,4]{1,2,0:T(4,128)(2,1)} fusion(bf16[8,4,2048]{0,1,2:T(4,128)(2,1)S(1)} %copy.24, s32[2048]{0:T(1024)S(1)} %fusion.15), kind=kCustom, calls=%fused_computation.1 | custom fusion | bytes 270336 | tf_op jit(solution)/shard_map/jit(_take)/gather | solution.py:47
  192.1 10.0 %fusion.17 = bf16[2048,4,8]{2,1,0:T(4,128)(2,1)S(1)} fusion(bf16[2048,8,4]{1,2,0:T(4,128)(2,1)} %gather_fusion.1, pred[2048]{0:T(1024)(128)(4,1)S(1)} %compare_and_fusion.1), kind=kLoop, calls=%fused_computation.64 | loop fusion | flops 65536 | bytes 264192
  202.1 2.9 reshape.84
  205.0 8.2 %all-to-all-start = ((bf16[16,2,2048]{2,1,0:T(2,128)(2,1)}), bf16[16,2,2048]{2,1,0:T(2,128)(2,1)S(1)}, u32[]{:S(2)}, u32[]{:S(2)}) async-start(bf16[16,2,2048]{2,1,0:T(2,128)(2,1)} %reshape.84), calls=%async_computation | async-start | bytes 262144 | tf_op jit(solution)/shard_map/all_to_all | solution.py:48
  214.0 7.1 %all-to-all-done = bf16[16,2,2048]{2,1,0:T(2,128)(2,1)S(1)} async-done(((bf16[16,2,2048]{2,1,0:T(2,128)(2,1)}), bf16[16,2,2048]{2,1,0:T(2,128)(2,1)S(1)}, u32[]{:S(2)}, u32[]{:S(2)}) %all-to-all-start) | async-done | bytes 131104 | tf_op jit(solution)/shard_map/all_to_all | solution.py:48
  221.1 2.4 reshape.85
  223.5 1.2 copy.25
  224.7 0.2 fusion.11
  224.9 0.9 convolution_bitcast_fusion
  225.9 0.6 dynamic-slice
  227.2 99.9 %all-reduce.4.cloned.1.call-done = f32[128,128]{1,0:T(8,128)} async-done(((f32[128,128]{1,0:T(8,128)}), f32[128,128]{1,0:T(8,128)}) %all-reduce.4.cloned.1.call-update) | async-done | bytes 65552
  327.0 1.3 constant_dynamic-slice_fusion.1
  (64 shorter events, 3.0 us)
Async XLA Ops:
  6.5 218.4 %copy-start = (bf16[128,4,4,128]{3,2,1,0:T(4,128)(2,1)S(1)}, bf16[128,4,4,128]{3,2,1,0:T(4,128)(2,1)}, u32[]{:S(2)}) copy-start(bf16[128,4,4,128]{3,2,1,0:T(4,128)(2,1)} %param.12) | copy-start | bytes 1572868
  205.0 16.0 %all-to-all-start = ((bf16[16,2,2048]{2,1,0:T(2,128)(2,1)}), bf16[16,2,2048]{2,1,0:T(2,128)(2,1)S(1)}, u32[]{:S(2)}, u32[]{:S(2)}) async-start(bf16[16,2,2048]{2,1,0:T(2,128)(2,1)} %reshape.84), calls=%async_computation | async-start | bytes 262144 | tf_op jit(solution)/shard_map/all_to_all | solution.py:48
  213.3 113.8 %all-reduce.4.cloned.1.call-start = ((), (), s32[]{:S(2)}) async-start(), calls=%async_computation.1 | async-start | bytes 131072
  224.7 1.2 copy-start.1
Sparse Core Ops, SparseCore 0:
  226.0 100.9 all-reduce.3
where the time goes:
time: 336 us; the launch traced here: 335 us
  other arithmetic  134 us (40%)
  waiting for transfers between devices  107 us (32%)
  local copies, waits for them, and re-layouts  67.1 us (20%)
  between operations  14.8 us (4%)
  starting transfers between devices  8.27 us (2%)
    reduce_sum x8, other arithmetic, one_time(): return jnp.sum(node_table[:, None, :] * values, axis=0).astype(jnp.bfloat16)  116 us
    unnamed x2, waiting for transfers between devices  99.9 us
    gather x8, local copies, waits for them, and re-layouts, one_time(): values = jnp.take(moment, elem_local, axis=2)  28.6 us
    gather x1, local copies, waits for them, and re-layouts, body(): outgoing = jnp.take(everything, order, axis=2)  14.5 us
    unnamed x1, other arithmetic  10 us
    dynamic_slice x16, local copies, waits for them, and re-layouts, body(): local_sources = lax.map(one_time, donor)  8.94 us
    all_to_all x1, starting transfers between devices, body(): lax.all_to_all(outgoing, 'panel', split_axis=2, concat_axis=0, tiled=True)  8.23 us
    unnamed x8, local copies, waits for them, and re-layouts  7.22 us
  transfers between devices with their start and end apart: 2, of which 2 were waited for; matrix products, arithmetic and copies ran while one was open for 0% of the time, Pallas kernels for 0%

commit v1 on v0

v1 whole, which is shorter than its diff:
```python
import functools

import jax
import jax.numpy as jnp
from jax import lax
from jax.experimental import pallas as pl
from jax.experimental.pallas import tpu as pltpu
from jax.sharding import PartitionSpec as P

LANES = 128
NODE_SPOTS = (-1.0, -0.5, 0.0, 0.5, 1.0)
VM = pl.BlockSpec(memory_space=pltpu.VMEM)
SM = pl.BlockSpec(memory_space=pltpu.SMEM)
NT = (((1,), (1,)), ((), ()))


def lagrange_rows(coord):
    rows = []
    for one in range(5):
        value = None
        scale = 1.0
        for two in range(5):
            if two != one:
                scale = scale * (NODE_SPOTS[one] - NODE_SPOTS[two])
                factor = coord - NODE_SPOTS[two]
                value = factor if value is None else value * factor
        rows.append(value * (1.0 / scale))
    return rows


def interpolate(shape, donor_ref, elem_ref, coords_ref, out_ref, table_ref, hold_ref):
    times, nodes, quants, elems = shape
    points = coords_ref.shape[1]
    width = 2 * LANES
    rows = nodes * quants
    groups = (rows + 7) // 8
    base = lax.axis_index("obs") * elems
    upper = lax.broadcasted_iota(jnp.int32, (8, width), 0) >= quants
    for tile in range(points // width):
        lanes = slice(tile * width, (tile + 1) * width)
        factors = [lagrange_rows(jnp.broadcast_to(coords_ref[d : d + 1, lanes], (8, width))) for d in range(3)]
        zero = jnp.zeros((8, width), jnp.float32)
        basis = []
        for a in range(5):
            for b in range(5):
                ab = factors[0][a] * factors[1][b]
                for c in range(5):
                    basis.append(ab * factors[2][c])
        padded = [zero] + basis + [zero]
        for m in range(groups):
            table_ref[0, m * 8 : m * 8 + 8, :] = jnp.where(upper, padded[2 * m + 2], padded[2 * m + 1])
            table_ref[1, m * 8 : m * 8 + 8, :] = jnp.where(upper, padded[2 * m + 1], padded[2 * m])
        ids = jnp.broadcast_to(elem_ref[0:1, lanes] - base, (elems, width))
        pick = jnp.where(ids == lax.broadcasted_iota(jnp.int32, (elems, width), 0), 1.0, 0.0).astype(jnp.bfloat16)
        for pair in range(times // 2):
            found = jnp.dot(
                donor_ref[pair * 2 * rows : (pair + 1) * 2 * rows, :], pick, preferred_element_type=jnp.float32
            )
            for odd in range(2):
                first = odd * (2 * rows - groups * 8)
                product = found[first : first + groups * 8, :] * table_ref[odd]
                total = jnp.sum(product.reshape(groups, 8, width), axis=0)
                total = total + pltpu.roll(total, 4, 0)
                for q in range(quants):
                    row = q * times + 2 * pair + odd
                    hold_ref[row : row + 1, lanes] = total[q : q + 1]
    out_ref[...] = hold_ref[...].astype(jnp.bfloat16)


def owned_rows(owner_row, src, n_panel):
    src = src.astype(jnp.float32)
    picked = [jnp.where(owner_row == p, src, 0.0).astype(jnp.bfloat16) for p in range(n_panel)]
    return jnp.concatenate(picked, axis=0)


def spots(pos_row, size):
    hit = lax.broadcasted_iota(jnp.int32, (size, pos_row.shape[1]), 0) == pos_row
    return jnp.where(hit, 1.0, 0.0).astype(jnp.bfloat16)


def place_own(n_panel, n_obs, src_ref, owner_ref, out_ref, pos_ref):
    points = src_ref.shape[1]
    every = owner_ref.shape[1]
    size = every // n_panel
    tiles = every // LANES
    spans = (n_panel, LANES)
    rows_p = lax.broadcasted_iota(jnp.int32, spans, 0)
    hits = [
        jnp.where(rows_p == owner_ref[0:1, c * LANES : (c + 1) * LANES], 1.0, 0.0) for c in range(tiles)
    ]
    left = lax.broadcasted_iota(jnp.int32, (LANES, 2 * LANES), 0)
    right = lax.broadcasted_iota(jnp.int32, (LANES, 2 * LANES), 1)
    count = jnp.where((left < right), 1.0, 0.0).astype(jnp.bfloat16)
    sums = jnp.dot(
        jnp.concatenate(hits, axis=0).astype(jnp.bfloat16), count, preferred_element_type=jnp.float32
    )
    before = jnp.zeros(spans, jnp.float32)
    for c in range(tiles):
        part = sums[c * n_panel : (c + 1) * n_panel]
        rank = jnp.sum(hits[c] * (part[:, :LANES] + before), axis=0, keepdims=True)
        pos_ref[0:1, c * LANES : (c + 1) * LANES] = rank.astype(jnp.int32)
        before = before + part[:, LANES:]
    at = pl.ds(pl.multiple_of(lax.axis_index("obs") * points, points), points)
    out_ref[...] = lax.dot_general(
        owned_rows(owner_ref[0:1, at], src_ref[...], n_panel),
        spots(pos_ref[0:1, at], size),
        NT,
        preferred_element_type=jnp.float32,
    ).astype(jnp.bfloat16)


def place_rest(n_panel, n_obs, part_ref, pos_ref, owner_ref, *refs):
    out_ref = refs[-1]
    points = refs[0].shape[1]
    size = owner_ref.shape[1] // n_panel
    total = part_ref[...].astype(jnp.float32)
    for step in range(1, n_obs):
        block = lax.rem(lax.axis_index("obs") + (n_obs - step), n_obs)
        at = pl.ds(pl.multiple_of(block * points, points), points)
        total = total + lax.dot_general(
            owned_rows(owner_ref[0:1, at], refs[step - 1][...], n_panel),
            spots(pos_ref[0:1, at], size),
            NT,
            preferred_element_type=jnp.float32,
        )
    out_ref[...] = total.astype(jnp.bfloat16).reshape(out_ref.shape)


def band_sum(quants, band, got_ref, weight_ref, offset_ref, out_ref, lag_ref, shift_ref):
    parts, rows, size = got_ref.shape
    times = rows // quants
    span = parts * times
    values = got_ref[...].astype(jnp.float32)
    flat = jnp.concatenate(
        [values[:, q * times : (q + 1) * times, :].reshape(span, size).astype(jnp.bfloat16) for q in range(quants)],
        axis=1,
    )
    total = None
    for k in range(band):
        one = lax.dot_general(flat, weight_ref[k], NT, preferred_element_type=jnp.float32)
        if k:
            lag_ref[k - 1, 0:8, :] = jnp.zeros((8, one.shape[1]), jnp.float32)
            lag_ref[k - 1, 8 : 8 + span, :] = one
            one = lag_ref[k - 1, 8 - k : 8 - k + span, :]
        total = one if total is None else total + one
    shift_ref[0:span, :] = jnp.zeros_like(total)
    shift_ref[span : 2 * span, :] = total
    out_ref[...] = shift_ref[pl.ds(span - offset_ref[0, 0], span), :].reshape(out_ref.shape)


def body(donor, donor_elem, local_coords, owner, weights, offsets):
    times, nodes, quants, elems = donor.shape
    points = local_coords.shape[1]
    every = owner.shape[0]
    n_panel = lax.axis_size("panel")
    n_obs = lax.axis_size("obs")
    size = every // n_panel
    observers, band = weights.shape[:2]
    rows = times * quants
    sources = pl.pallas_call(
        functools.partial(interpolate, donor.shape),
        out_shape=jax.ShapeDtypeStruct((rows, points), jnp.bfloat16),
        in_specs=[VM, VM, VM],
        out_specs=VM,
        scratch_shapes=[
            pltpu.VMEM((2, 8 * ((nodes * quants + 7) // 8), 2 * LANES), jnp.float32),
            pltpu.VMEM((rows, points), jnp.float32),
        ],
        name="interpolate",
    )(donor.reshape(times * nodes * quants, elems), donor_elem.reshape(1, points), local_coords)
    others = [
        lax.ppermute(sources, "obs", [(s, (s + step) % n_obs) for s in range(n_obs)]) for step in range(1, n_obs)
    ]
    owner_row = owner.reshape(1, every)
    part, pos = pl.pallas_call(
        functools.partial(place_own, n_panel, n_obs),
        out_shape=(
            jax.ShapeDtypeStruct((n_panel * rows, size), jnp.bfloat16),
            jax.ShapeDtypeStruct((1, every), jnp.int32),
        ),
        in_specs=[VM, VM],
        out_specs=(VM, VM),
        name="place_own",
    )(sources, owner_row)
    outgoing = pl.pallas_call(
        functools.partial(place_rest, n_panel, n_obs),
        out_shape=jax.ShapeDtypeStruct((n_panel, rows, size), jnp.bfloat16),
        in_specs=[VM] * (2 + n_obs),
        out_specs=VM,
        name="place_rest",
    )(part, pos, owner_row, *others)
    got = lax.all_to_all(outgoing, "panel", split_axis=0, concat_axis=0, tiled=True)
    weight_rows = weights.transpose(1, 0, 2, 3).reshape(band, observers, quants * size)
    span = n_panel * times
    partial = pl.pallas_call(
        functools.partial(band_sum, quants, band),
        out_shape=jax.ShapeDtypeStruct((n_panel, times, observers), jnp.float32),
        in_specs=[VM, VM, SM],
        out_specs=VM,
        scratch_shapes=[
            pltpu.VMEM((band - 1, 8 + span, observers), jnp.float32),
            pltpu.VMEM((2 * span, observers), jnp.float32),
        ],
        name="band_sum",
    )(got, weight_rows, offsets)
    shares = lax.all_to_all(partial, "panel", split_axis=0, concat_axis=0, tiled=True)
    return jnp.sum(shares, axis=0)


def solution(mesh):
    return jax.shard_map(
        body,
        mesh=mesh,
        in_specs=(
            P("panel", None, None, "obs"),
            P("obs"),
            P(None, "obs"),
            P(),
            P("obs", None, None, "panel"),
            P("obs", "panel"),
        ),
        out_specs=P("panel", "obs"),
        check_vma=False,
    )
```

time: 336 us -> 40.3 us (0.12)
  other arithmetic: 134 us -> 0.61 us
  waiting for transfers between devices: 107 us -> 6.3 us
  local copies, waits for them, and re-layouts: 67.1 us -> 2.37 us
  between operations: 14.8 us -> 0.68 us
  Pallas kernels: 0 us -> 10.6 us
  blocking collectives: 2.01 us -> 11 us
    reduce_sum x8 -> x1, other arithmetic: 116 us -> 0.61 us  [body(): return jnp.sum(shares, axis=0)]
    unnamed x2 -> x0, waiting for transfers between devices: 99.9 us -> none
    gather x9 -> x0, local copies, waits for them, and re-layouts: 43.1 us -> none  [the longest x8 28.6 us: one_time(): values = jnp.take(moment, elem_local, axis=2)]
    all_to_all x0 -> x1, blocking collectives: none -> 11 us  [body(): lax.all_to_all(partial, 'panel', split_axis=0, concat_axis=0, tiled=True)]
    pallas_call x0 -> x4, Pallas kernels: none -> 10.6 us  [the longest x1 4.34 us: body(): pl.pallas_call(functools.partial(interpolate, donor.shape), out_shape=jax...]
    unnamed x1 -> x0, other arithmetic: 10 us -> none
    dynamic_slice x16 -> x0, local copies, waits for them, and re-layouts: 8.94 us -> none  [body(): local_sources = lax.map(one_time, donor)]
    unnamed x8 -> x6, local copies, waits for them, and re-layouts: 7.22 us -> 1.28 us
  transfers between devices with their start and end apart: 2 -> 2, of which waited for: 2 -> 1; matrix products, arithmetic and copies ran while one was open for 0% -> 3% of each run, Pallas kernels for 0% -> 5%
where the time goes in v1:
time: 40.3 us; the launch traced here: 40 us
  blocking collectives  11 us (27%)
  Pallas kernels  10.6 us (26%)
  starting transfers between devices  8.4 us (21%)
  waiting for transfers between devices  6.3 us (16%)
  local copies, waits for them, and re-layouts  2.37 us (6%)
  between operations  0.68 us (2%)
  other arithmetic  0.61 us (2%)
    all_to_all x1, blocking collectives, body(): lax.all_to_all(partial, 'panel', split_axis=0, concat_axis=0, tiled=True)  11 us
    all_to_all x1, starting transfers between devices, body(): lax.all_to_all(outgoing, 'panel', split_axis=0, concat_axis=0, tiled=True)  7.9 us
    all_to_all x1, waiting for transfers between devices, body(): lax.all_to_all(outgoing, 'panel', split_axis=0, concat_axis=0, tiled=True)  6.3 us
    pallas_call x1, Pallas kernels, body(): pl.pallas_call(functools.partial(interpolate, donor.shape), out_shape=jax...  4.34 us
    pallas_call x1, Pallas kernels, body(): pl.pallas_call(functools.partial(place_own, n_panel, n_obs), out_shape=(j...  2.18 us
    pallas_call x1, Pallas kernels, body(): pl.pallas_call(functools.partial(band_sum, quants, band), out_shape=jax.S...  2.06 us
    pallas_call x1, Pallas kernels, body(): pl.pallas_call(functools.partial(place_rest, n_panel, n_obs), out_shape=j...  2.03 us
    unnamed x6, local copies, waits for them, and re-layouts  1.28 us
  transfers between devices with their start and end apart: 2, of which 1 were waited for; matrix products, arithmetic and copies ran while one was open for 3% of the time, Pallas kernels for 5%

profile of v1, /device:TPU:0, one launch (start us, length us, event | category | flops | bytes accessed | tf_op | source)
XLA Modules:
  0.0 40.0 jit_solution(6104960388331556295)
XLA Ops:
  0.0 4.3 %interpolate.1.src_ref = bf16[32,1024]{1,0:T(8,128)(2,1)} custom-call(bf16[4000,128]{1,0:T(8,128)(2,1)} %bitcast.6, s32[1,1024]{1,0:T(1,128)} %bitcast.10, f32[3,1024]{1,0:T(4,128)} %coords_ref.1), custom_call_target="tpu_custom_call" | custom-call | tf_op jit(solution)/shard_map/interpolate/pallas_call | solution.py:160
  4.3 0.0 copy-start.1
  4.3 0.5 %collective-permute-start = (bf16[32,1024]{1,0:T(8,128)(2,1)}, bf16[32,1024]{1,0:T(8,128)(2,1)S(1)}, u32[]{:S(2)}, u32[]{:S(2)}) collective-permute-start(bf16[32,1024]{1,0:T(8,128)(2,1)} %interpolate.1.src_ref), channel_id=1, source_target_pairs={{0,1},{1,0},{2,3},{3,2},{4,5},{5,4},{6,7},{7,6},{8,9},{9,8},{10,11... | collective-permute-start | bytes 196616 | tf_op jit(solution)/shard_map/ppermute | solution.py:172
  4.8 2.2 %place_own.1 = (bf16[512,128]{1,0:T(8,128)(2,1)}, s32[1,2048]{1,0:T(1,128)}) custom-call(bf16[32,1024]{1,0:T(8,128)(2,1)} %interpolate.1.src_ref, s32[1,2048]{1,0:T(1,128)} %bitcast.8), custom_call_target="tpu_custom_call" | custom-call | tf_op jit(solution)/shard_map/place_own/pallas_call | solution.py:175
  7.0 0.0 collective-permute-done.refs_0_
  7.0 0.0 copy-start.2
  7.0 0.6 %copy-done.2 = bf16[32,1024]{1,0:T(8,128)(2,1)} copy-done((bf16[32,1024]{1,0:T(8,128)(2,1)}, bf16[32,1024]{1,0:T(8,128)(2,1)S(1)}, u32[]{:S(2)}) %copy-start.2) | copy-done | bytes 65560
  7.7 2.0 %place_rest.1 = bf16[16,32,128]{2,1,0:T(8,128)(2,1)} custom-call(bf16[512,128]{1,0:T(8,128)(2,1)} %get-tuple-element.7.part_ref, s32[1,2048]{1,0:T(1,128)} %get-tuple-element.8.pos_ref, s32[1,2048]{1,0:T(1,128)} %bitcast.9, bf16[32,1024]{1,0:T(8,128)(2,1)} %copy-done.2), custom_call_target="tpu_custom_call" | custom-call | tf_op jit(solution)/shard_map/place_rest/pallas_call | solution.py:185
  9.7 7.9 %all-to-all-start = ((bf16[16,32,128]{2,1,0:T(8,128)(2,1)}), bf16[16,32,128]{2,1,0:T(8,128)(2,1)S(1)}, u32[]{:S(2)}, u32[]{:S(2)}) async-start(bf16[16,32,128]{2,1,0:T(8,128)(2,1)} %place_rest.1), calls=%async_computation | async-start | bytes 262144 | tf_op jit(solution)/shard_map/all_to_all | solution.py:192
  17.6 0.0 copy-done.1
  17.6 0.2 reshape.16
  17.8 0.9 %copy.8.weight_ref = bf16[4,128,512]{2,1,0:T(8,128)(2,1)} copy(bf16[4,128,512]{2,0,1:T(4,128)(2,1)S(1)} %reshape.16) | data formatting | bytes 1048576 | tf_op jit(solution)/shard_map/reshape | solution.py:193
  19.4 6.3 %all-to-all-done.got_ref = bf16[16,32,128]{2,1,0:T(8,128)(2,1)S(1)} async-done(((bf16[16,32,128]{2,1,0:T(8,128)(2,1)}), bf16[16,32,128]{2,1,0:T(8,128)(2,1)S(1)}, u32[]{:S(2)}, u32[]{:S(2)}) %all-to-all-start) | async-done | bytes 131104 | tf_op jit(solution)/shard_map/all_to_all | solution.py:192
  25.7 0.0 copy-start
  25.7 0.6 %copy-done = bf16[16,32,128]{2,1,0:T(8,128)(2,1)} copy-done((bf16[16,32,128]{2,1,0:T(8,128)(2,1)}, bf16[16,32,128]{2,1,0:T(8,128)(2,1)S(1)}, u32[]{:S(2)}) %copy-start) | copy-done | bytes 131096
  26.3 2.1 %band_sum.1 = f32[16,8,128]{2,1,0:T(8,128)} custom-call(bf16[16,32,128]{2,1,0:T(8,128)(2,1)} %copy-done, bf16[4,128,512]{2,1,0:T(8,128)(2,1)} %copy.8.weight_ref, s32[1,1]{1,0:T(1,128)S(6)} %copy.9.offset_ref), custom_call_target="tpu_custom_call" | custom-call | tf_op jit(solution)/shard_map/band_sum/pallas_call | solution.py:195
  28.4 11.0 %all_to_all.10 = f32[16,8,128]{2,1,0:T(8,128)S(1)} all-to-all(f32[16,8,128]{2,1,0:T(8,128)} %band_sum.1), channel_id=1, replica_groups=mesh['panel'=16,'obs'=2] {'panel'}, dimensions={0} | all-to-all | bytes 131072 | tf_op jit(solution)/shard_map/all_to_all | solution.py:206
  39.4 0.6 %reduce_sum.9 = f32[8,128]{1,0:T(8,128)} reduce(f32[16,8,128]{2,1,0:T(8,128)S(1)} %all_to_all.10, f32[]{:T(128)} %constant.0.clone.1), dimensions={0}, to_apply=%region_0.0 | reduce | flops 15360 | bytes 69636 | tf_op jit(solution)/shard_map/reduce_sum | solution.py:207
Async XLA Ops:
  4.3 13.3 %copy-start.1 = (bf16[128,4,4,128]{3,2,1,0:T(4,128)(2,1)S(1)}, bf16[128,4,4,128]{3,2,1,0:T(4,128)(2,1)}, u32[]{:S(2)}) copy-start(bf16[128,4,4,128]{3,2,1,0:T(4,128)(2,1)} %param.10) | copy-start | bytes 1572868
  4.3 2.7 %collective-permute-start = (bf16[32,1024]{1,0:T(8,128)(2,1)}, bf16[32,1024]{1,0:T(8,128)(2,1)S(1)}, u32[]{:S(2)}, u32[]{:S(2)}) collective-permute-start(bf16[32,1024]{1,0:T(8,128)(2,1)} %interpolate.1.src_ref), channel_id=1, source_target_pairs={{0,1},{1,0},{2,3},{3,2},{4,5},{5,4},{6,7},{7,6},{8,9},{9,8},{10,11... | collective-permute-start | bytes 196616 | tf_op jit(solution)/shard_map/ppermute | solution.py:172
  7.0 0.6 %copy-start.2 = (bf16[32,1024]{1,0:T(8,128)(2,1)}, bf16[32,1024]{1,0:T(8,128)(2,1)S(1)}, u32[]{:S(2)}) copy-start(bf16[32,1024]{1,0:T(8,128)(2,1)S(1)} %collective-permute-done.refs_0_) | copy-start | bytes 196612
  9.7 16.0 %all-to-all-start = ((bf16[16,32,128]{2,1,0:T(8,128)(2,1)}), bf16[16,32,128]{2,1,0:T(8,128)(2,1)S(1)}, u32[]{:S(2)}, u32[]{:S(2)}) async-start(bf16[16,32,128]{2,1,0:T(8,128)(2,1)} %place_rest.1), calls=%async_computation | async-start | bytes 262144 | tf_op jit(solution)/shard_map/all_to_all | solution.py:192
  25.7 0.6 %copy-start = (bf16[16,32,128]{2,1,0:T(8,128)(2,1)}, bf16[16,32,128]{2,1,0:T(8,128)(2,1)S(1)}, u32[]{:S(2)}) copy-start(bf16[16,32,128]{2,1,0:T(8,128)(2,1)S(1)} %all-to-all-done.got_ref) | copy-start | bytes 393220

commit v2 on v1

v2 whole, which is shorter than its diff:
```python
import functools

import jax
import jax.numpy as jnp
from jax import lax
from jax.experimental import pallas as pl
from jax.experimental.pallas import tpu as pltpu
from jax.sharding import PartitionSpec as P

LANES = 128
SHUFFLED = 36
NODE_SPOTS = (-1.0, -0.5, 0.0, 0.5, 1.0)
VM = pl.BlockSpec(memory_space=pltpu.VMEM)
SM = pl.BlockSpec(memory_space=pltpu.SMEM)
NT = (((1,), (1,)), ((), ()))


def near(x):
    return pltpu.with_memory_space_constraint(x, pltpu.VMEM)


def lagrange_rows(coords):
    rows = []
    for one in range(5):
        value = None
        scale = 1.0
        for two in range(5):
            if two != one:
                scale = scale * (NODE_SPOTS[one] - NODE_SPOTS[two])
                factor = coords - NODE_SPOTS[two]
                value = factor if value is None else value * factor
        rows.append(value * (1.0 / scale))
    return rows


def interpolate(shape, shuffled, n_panel, donor_src, elem_src, coords_src, owner_src, out_ref, pos_ref, chunk_ref, elem_ref, coords_ref, owner_ref, wide_ref, table_ref, hold_ref, sems):
    times, nodes, quants, elems = shape
    points = coords_ref.shape[1]
    width = 2 * LANES
    rows = nodes * quants
    groups = (rows + 7) // 8
    pairs = times // 2
    half = pairs // 2 * 2 * rows
    copies = [
        pltpu.make_async_copy(donor_src.at[pl.ds(0, half), :], chunk_ref.at[pl.ds(0, half), :], sems.at[0]),
        pltpu.make_async_copy(
            donor_src.at[pl.ds(half, times * rows - half), :], chunk_ref.at[pl.ds(half, times * rows - half), :], sems.at[4]
        ),
    ]
    first = pltpu.make_async_copy(coords_src, coords_ref, sems.at[1])
    second = pltpu.make_async_copy(elem_src, elem_ref, sems.at[2])
    third = pltpu.make_async_copy(owner_src, owner_ref, sems.at[3])
    first.start()
    second.start()
    third.start()
    for copy in copies:
        copy.start()
    first.wait()
    second.wait()
    third.wait()
    rank_points(n_panel, owner_ref, pos_ref)
    base = lax.axis_index("obs") * elems
    upper = lax.broadcasted_iota(jnp.int32, (8, width), 0) >= quants
    tables = lagrange_rows(coords_ref[...])
    zero = jnp.zeros((8, width), jnp.float32)
    for tile in range(points // width):
        lanes = slice(tile * width, (tile + 1) * width)
        factors = [
            [jnp.broadcast_to(tables[a][d : d + 1, lanes], (8, width)) for a in range(5)] for d in range(3)
        ]
        ab = [factors[0][n // 5] * factors[1][n % 5] for n in range(25)]
        lasts = factors[2]
        mixed = {(c, (c + 1) % 5): jnp.where(upper, lasts[(c + 1) % 5], lasts[c]) for c in range(5)}
        for odd in range(2):
            for m in range(groups):
                low, high = 2 * m - odd, 2 * m - odd + 1
                if low < 0:
                    value = jnp.where(upper, ab[0] * lasts[0], zero)
                elif high >= nodes:
                    value = jnp.where(upper, zero, ab[-1] * lasts[-1])
                else:
                    front = ab[low // 5]
                    if high // 5 != low // 5:
                        front = jnp.where(upper, ab[high // 5], front)
                    value = front * mixed[(low % 5, high % 5)]
                table_ref[odd, m * 8 : m * 8 + 8, :] = value
        ids = elem_ref[0:1, lanes] - base
        wanted = jnp.broadcast_to(ids, (elems, width))
        pick = jnp.where(wanted == lax.broadcasted_iota(jnp.int32, (elems, width), 0), 1.0, 0.0).astype(jnp.bfloat16)
        for pair in range(pairs):
            if tile == 0 and pair % (pairs // 2) == 0:
                copies[pair // (pairs // 2)].wait()
                if shuffled:
                    for p in range(pair, pair + pairs // 2):
                        wide_ref[p] = chunk_ref[2 * rows * p : 2 * rows * p + 8 * shuffled, :].astype(jnp.float32)
            found = jnp.dot(
                chunk_ref[2 * rows * pair + 8 * shuffled : 2 * rows * (pair + 1), :], pick, preferred_element_type=jnp.float32)
            if shuffled:
                halves = [
                    jnp.take_along_axis(
                        wide_ref[pair],
                        jnp.broadcast_to(ids[:, h * LANES : (h + 1) * LANES], (8 * shuffled, LANES)),
                        axis=1,
                        mode="promise_in_bounds",
                    )
                    for h in range(2)
                ]
                found = jnp.concatenate([jnp.concatenate(halves, axis=1), found], axis=0)
            for odd in range(2):
                start = odd * (2 * rows - groups * 8)
                product = found[start : start + groups * 8, :] * table_ref[odd]
                total = jnp.sum(product.reshape(groups, 8, width), axis=0)
                total = total + pltpu.roll(total, 4, 0)
                for q in range(quants):
                    row = q * times + 2 * pair + odd
                    hold_ref[row : row + 1, lanes] = total[q : q + 1]
    out_ref[...] = hold_ref[...].astype(jnp.bfloat16)


def place(owner_row, pos_row, src, n_panel, size):
    src = src.astype(jnp.float32)
    half = lax.shift_right_logical(owner_row, 1)
    picked = [jnp.where(half == p, src, 0.0).astype(jnp.bfloat16) for p in range(n_panel // 2)]
    spot = pos_row + (owner_row - 2 * half) * size
    hit = lax.broadcasted_iota(jnp.int32, (2 * size, spot.shape[1]), 0) == spot
    hot = jnp.where(hit, 1.0, 0.0).astype(jnp.bfloat16)
    return lax.dot_general(jnp.concatenate(picked, axis=0), hot, NT, preferred_element_type=jnp.float32)


def rank_points(n_panel, owner_ref, pos_ref):
    every = owner_ref.shape[1]
    tiles = every // LANES
    spans = (n_panel, LANES)
    rows_p = lax.broadcasted_iota(jnp.int32, spans, 0)
    hits = [
        jnp.where(rows_p == owner_ref[0:1, c * LANES : (c + 1) * LANES], 1.0, 0.0) for c in range(tiles)
    ]
    left = lax.broadcasted_iota(jnp.int32, (LANES, 2 * LANES), 0)
    right = lax.broadcasted_iota(jnp.int32, (LANES, 2 * LANES), 1)
    count = jnp.where((left < right), 1.0, 0.0).astype(jnp.bfloat16)
    sums = jnp.dot(
        jnp.concatenate(hits, axis=0).astype(jnp.bfloat16), count, preferred_element_type=jnp.float32
    )
    before = jnp.zeros(spans, jnp.float32)
    for c in range(tiles):
        part = sums[c * n_panel : (c + 1) * n_panel]
        rank = jnp.sum(hits[c] * (part[:, :LANES] + before), axis=0, keepdims=True)
        pos_ref[0:1, c * LANES : (c + 1) * LANES] = rank.astype(jnp.int32)
        before = before + part[:, LANES:]


def place_own(n_panel, src_ref, owner_ref, pos_ref, weight_ref, out_ref, sorted_ref, wide_ref):
    points = src_ref.shape[1]
    size = owner_ref.shape[1] // n_panel
    band, observers, width = sorted_ref.shape
    quants = width // size
    wide_ref[...] = weight_ref[...].astype(jnp.float32)
    for k in range(band):
        for q in range(quants):
            lane = pl.ds(k * quants + q, observers, stride=band * quants)
            sorted_ref[k, :, q * size : (q + 1) * size] = wide_ref[lane, :].astype(jnp.bfloat16)
    at = pl.ds(pl.multiple_of(lax.axis_index("obs") * points, points), points)
    out_ref[...] = place(owner_ref[0:1, at], pos_ref[0:1, at], src_ref[...], n_panel, size).astype(jnp.bfloat16)


def place_rest(n_panel, n_obs, part_ref, owner_ref, pos_ref, offset_ref, *refs):
    others, (out_ref, delay_ref) = refs[:-2], refs[-2:]
    rows, points = others[0].shape
    size = owner_ref.shape[1] // n_panel
    delay_ref[...] = jnp.full(delay_ref.shape, offset_ref[0, 0].astype(jnp.float32))
    total = part_ref[...].astype(jnp.float32)
    for step in range(1, n_obs):
        block = lax.rem(lax.axis_index("obs") + (n_obs - step), n_obs)
        at = pl.ds(pl.multiple_of(block * points, points), points)
        total = total + place(owner_ref[0:1, at], pos_ref[0:1, at], others[step - 1][...], n_panel, size)
    total = total.astype(jnp.bfloat16)
    for p in range(n_panel):
        out_ref[p] = total[p // 2 * rows : (p // 2 + 1) * rows, p % 2 * size : (p % 2 + 1) * size]


def band_sum(quants, band, got_ref, weight_ref, delay_ref, out_ref, lag_ref, shift_ref):
    parts, rows, size = got_ref.shape
    times = rows // quants
    span = parts * times
    values = got_ref[...].astype(jnp.float32)
    flat = jnp.concatenate(
        [values[:, q * times : (q + 1) * times, :].reshape(span, size).astype(jnp.bfloat16) for q in range(quants)],
        axis=1,
    )
    total = None
    for k in range(band):
        one = lax.dot_general(flat, weight_ref[k], NT, preferred_element_type=jnp.float32)
        if k:
            lag_ref[k - 1, 0:8, :] = jnp.zeros((8, one.shape[1]), jnp.float32)
            lag_ref[k - 1, 8 : 8 + span, :] = one
            one = lag_ref[k - 1, 8 - k : 8 - k + span, :]
        total = one if total is None else total + one
    shift_ref[0:span, :] = jnp.zeros_like(total)
    shift_ref[span : 2 * span, :] = total
    out_ref[...] = shift_ref[pl.ds(span - jnp.max(delay_ref[...]).astype(jnp.int32), span), :].reshape(out_ref.shape)


def body(donor, donor_elem, local_coords, owner, weights, offsets):
    times, nodes, quants, elems = donor.shape
    points = local_coords.shape[1]
    every = owner.shape[0]
    n_panel = lax.axis_size("panel")
    n_obs = lax.axis_size("obs")
    size = every // n_panel
    observers, band = weights.shape[:2]
    rows = times * quants
    owner_row = owner.reshape(1, every)
    sources, pos = pl.pallas_call(
        functools.partial(interpolate, donor.shape, SHUFFLED, n_panel),
        out_shape=(pltpu.VMEM((rows, points), jnp.bfloat16), pltpu.VMEM((1, every), jnp.int32)),
        in_specs=[pl.BlockSpec(memory_space=pl.ANY)] * 4,
        out_specs=(VM, VM),
        scratch_shapes=[
            pltpu.VMEM((times * nodes * quants, elems), jnp.bfloat16),
            pltpu.VMEM((1, points), jnp.int32),
            pltpu.VMEM(local_coords.shape, jnp.float32),
            pltpu.VMEM((1, every), jnp.int32),
            pltpu.VMEM((times // 2, 8 * max(SHUFFLED, 1), elems), jnp.float32),
            pltpu.VMEM((2, 8 * ((nodes * quants + 7) // 8), 2 * LANES), jnp.float32),
            pltpu.VMEM((rows, points), jnp.float32),
            pltpu.SemaphoreType.DMA((5,)),
        ],
        name="interpolate",
    )(donor.reshape(times * nodes * quants, elems), donor_elem.reshape(1, points), local_coords, owner_row)
    others = [
        lax.ppermute(sources, "obs", [(s, (s + step) % n_obs) for s in range(n_obs)]) for step in range(1, n_obs)
    ]
    part, weight_rows = pl.pallas_call(
        functools.partial(place_own, n_panel),
        out_shape=(
            pltpu.VMEM((n_panel // 2 * rows, 2 * size), jnp.bfloat16),
            pltpu.VMEM((band, observers, quants * size), jnp.bfloat16),
        ),
        in_specs=[VM, VM, VM, VM],
        out_specs=(VM, VM),
        scratch_shapes=[pltpu.VMEM((observers * band * quants, size), jnp.float32)],
        name="place_own",
    )(near(sources), near(owner_row), near(pos), near(weights.reshape(observers * band * quants, size)))
    outgoing, delay = pl.pallas_call(
        functools.partial(place_rest, n_panel, n_obs),
        out_shape=(pltpu.VMEM((n_panel, rows, size), jnp.bfloat16), pltpu.VMEM((1, LANES), jnp.float32)),
        in_specs=[VM, VM, VM, SM] + [VM] * (n_obs - 1),
        out_specs=(VM, VM),
        name="place_rest",
    )(near(part), near(owner_row), near(pos), offsets, *[near(x) for x in others])
    got = lax.all_to_all(outgoing, "panel", split_axis=0, concat_axis=0, tiled=True)
    span = n_panel * times
    partial = pl.pallas_call(
        functools.partial(band_sum, quants, band),
        out_shape=pltpu.VMEM((n_panel, times, observers), jnp.float32),
        in_specs=[VM, VM, VM],
        out_specs=VM,
        scratch_shapes=[
            pltpu.VMEM((band - 1, 8 + span, observers), jnp.float32),
            pltpu.VMEM((2 * span, observers), jnp.float32),
        ],
        name="band_sum",
    )(near(got), near(weight_rows), near(delay))
    shares = lax.all_to_all(partial, "panel", split_axis=0, concat_axis=0, tiled=True)
    return jnp.sum(shares, axis=0)


def solution(mesh):
    return jax.shard_map(
        body,
        mesh=mesh,
        in_specs=(
            P("panel", None, None, "obs"),
            P("obs"),
            P(None, "obs"),
            P(),
            P("obs", None, None, "panel"),
            P("obs", "panel"),
        ),
        out_specs=P("panel", "obs"),
        check_vma=False,
    )
```

time: 40.3 us -> 33 us (0.82)
  blocking collectives: 11 us -> 26.3 us
  starting transfers between devices: 8.4 us -> 0.54 us
  waiting for transfers between devices: 6.3 us -> 0.01 us
  Pallas kernels: 10.6 us -> 4.66 us
  local copies, waits for them, and re-layouts: 2.37 us -> 0.01 us
    all_to_all x0 -> x1, blocking collectives: none -> 15.8 us  [body(): lax.all_to_all(outgoing, 'panel', split_axis=0, concat_axis=0, tiled=True)]
    all_to_all x1 -> x0, starting transfers between devices: 7.9 us -> none  [body(): lax.all_to_all(outgoing, 'panel', split_axis=0, concat_axis=0, tiled=True)]
    all_to_all x1 -> x0, waiting for transfers between devices: 6.3 us -> none  [body(): lax.all_to_all(outgoing, 'panel', split_axis=0, concat_axis=0, tiled=True)]
    pallas_call x4, Pallas kernels: 10.6 us -> 4.66 us  [the longest x1 3.18 us: body(): pl.pallas_call(functools.partial(interpolate, donor.shape, SHUFFLED, n_pa...]
    unnamed x6 -> x4, local copies, waits for them, and re-layouts: 1.28 us -> 0.01 us
    reshape x2 -> x0, local copies, waits for them, and re-layouts: 1.09 us -> none  [body(): weights.transpose(1, 0, 2, 3).reshape(band, observers, quants * size)]
    all_to_all x1, blocking collectives: 11 us -> 10.5 us  [body(): lax.all_to_all(partial, 'panel', split_axis=0, concat_axis=0, tiled=True)]
  transfers between devices with their start and end apart: 2 -> 1, of which waited for: 1 -> 0; matrix products, arithmetic and copies ran while one was open for 3% -> 0% of each run, Pallas kernels for 5% -> 2%
where the time goes in v2:
time: 33 us; the launch traced here: 32.8 us
  blocking collectives  26.3 us (80%)
  Pallas kernels  4.66 us (14%)
  between operations  0.71 us (2%)
  other arithmetic  0.61 us (2%)
  starting transfers between devices  0.54 us (2%)
    all_to_all x1, blocking collectives, body(): lax.all_to_all(outgoing, 'panel', split_axis=0, concat_axis=0, tiled=True)  15.8 us
    all_to_all x1, blocking collectives, body(): lax.all_to_all(partial, 'panel', split_axis=0, concat_axis=0, tiled=True)  10.5 us
    pallas_call x1, Pallas kernels, body(): pl.pallas_call(functools.partial(interpolate, donor.shape, SHUFFLED, n_pa...  3.18 us
    pallas_call x1, Pallas kernels, body(): pl.pallas_call(functools.partial(place_own, n_panel), out_shape=(pltpu.VM...  0.77 us
  transfers between devices with their start and end apart: 1, of which 0 were waited for; matrix products, arithmetic and copies ran while one was open for 0% of the time, Pallas kernels for 2%

profile of v2, /device:TPU:0, one launch (start us, length us, event | category | flops | bytes accessed | tf_op | source)
XLA Modules:
  0.0 32.8 jit_solution(16140995865482374120)
XLA Ops:
  0.0 0.0 copy-start
  0.0 0.0 copy-start.1
  0.0 3.2 %interpolate.1 = (bf16[32,1024]{1,0:T(8,128)(2,1)S(1)}, s32[1,2048]{1,0:T(1,128)S(1)}) custom-call(bf16[4000,128]{1,0:T(8,128)(2,1)} %bitcast.8, s32[1,1024]{1,0:T(1,128)} %bitcast.9, f32[3,1024]{1,0:T(4,128)} %coords_src.1, s32[1,2048]{1,0:T(1,128)} %bitcast.5), custom_call_target="tpu_custom_call" | custom-call | tf_op jit(solution)/shard_map/interpolate/pallas_call | solution.py:213
  3.2 0.5 %collective-permute-start = (bf16[32,1024]{1,0:T(8,128)(2,1)S(1)}, bf16[32,1024]{1,0:T(8,128)(2,1)S(1)}, u32[]{:S(2)}, u32[]{:S(2)}) collective-permute-start(bf16[32,1024]{1,0:T(8,128)(2,1)S(1)} %get-tuple-element.11.src_ref), channel_id=1, source_target_pairs={{0,1},{1,0},{2,3},{3,2},{4,5},{5,4},{6,7},{7,6},{8,9},{9,8},{10,11... | collective-permute-start | bytes 196616 | tf_op jit(solution)/shard_map/ppermute | solution.py:231
  4.4 0.0 copy-done
  4.4 0.0 copy-done.1
  4.4 0.8 %place_own.1 = (bf16[256,256]{1,0:T(8,128)(2,1)S(1)}, bf16[4,128,512]{2,1,0:T(8,128)(2,1)S(1)}) custom-call(bf16[32,1024]{1,0:T(8,128)(2,1)S(1)} %get-tuple-element.11.src_ref, s32[1,2048]{1,0:T(1,128)S(1)} %bitcast.6, s32[1,2048]{1,0:T(1,128)S(1)} %get-tuple-element.12.pos_ref, bf16[2048,128]{1,0:T(8,128)(2,1)S(1)} %bitcast.4), custom_call_target="tpu_custom_call" | custom-call | tf_op jit(solution)/shard_map/place_own/pallas_call | solution.py:233
  5.2 0.0 collective-permute-done.refs_0_
  5.2 0.4 %place_rest.1 = (bf16[16,32,128]{2,1,0:T(8,128)(2,1)S(1)}, f32[1,128]{1,0:T(1,128)S(1)}) custom-call(bf16[256,256]{1,0:T(8,128)(2,1)S(1)} %get-tuple-element.13.part_ref, s32[1,2048]{1,0:T(1,128)S(1)} %bitcast.7, s32[1,2048]{1,0:T(1,128)S(1)} %get-tuple-element.12.pos_ref, s32[1,1]{1,0:T(1,128)S(6)} %copy.7.offset_ref, ...), custom_call_target="tpu_custom_call" | custom-call | tf_op jit(solution)/shard_map/place_rest/pallas_call | solution.py:244
  5.6 15.8 %all_to_all.10.got_ref = bf16[16,32,128]{2,1,0:T(8,128)(2,1)S(1)} all-to-all(bf16[16,32,128]{2,1,0:T(8,128)(2,1)S(1)} %get-tuple-element.14), channel_id=1, replica_groups=mesh['panel'=16,'obs'=2] {'panel'}, dimensions={0} | all-to-all | bytes 262144 | tf_op jit(solution)/shard_map/all_to_all | solution.py:251
  21.4 0.3 band_sum.1
  21.7 10.5 %all_to_all.11 = f32[16,8,128]{2,1,0:T(8,128)S(1)} all-to-all(f32[16,8,128]{2,1,0:T(8,128)S(1)} %band_sum.1), channel_id=1, replica_groups=mesh['panel'=16,'obs'=2] {'panel'}, dimensions={0} | all-to-all | bytes 131072 | tf_op jit(solution)/shard_map/all_to_all | solution.py:264
  32.2 0.6 %reduce_sum.9 = f32[8,128]{1,0:T(8,128)} reduce(f32[16,8,128]{2,1,0:T(8,128)S(1)} %all_to_all.11, f32[]{:T(128)} %constant.0.clone.1), dimensions={0}, to_apply=%region_0.0 | reduce | flops 15360 | bytes 69636 | tf_op jit(solution)/shard_map/reduce_sum | solution.py:265
Async XLA Ops:
  0.0 4.4 %copy-start = (bf16[128,4,4,128]{3,2,1,0:T(4,128)(2,1)S(1)}, bf16[128,4,4,128]{3,2,1,0:T(4,128)(2,1)}, u32[]{:S(2)}) copy-start(bf16[128,4,4,128]{3,2,1,0:T(4,128)(2,1)} %param.10) | copy-start | bytes 1572868
  0.0 4.4 %copy-start.1 = (s32[2048]{0:T(1024)S(1)}, s32[2048]{0:T(1024)}, u32[]{:S(2)}) copy-start(s32[2048]{0:T(1024)} %param.9) | copy-start | bytes 24580
  3.2 2.0 %collective-permute-start = (bf16[32,1024]{1,0:T(8,128)(2,1)S(1)}, bf16[32,1024]{1,0:T(8,128)(2,1)S(1)}, u32[]{:S(2)}, u32[]{:S(2)}) collective-permute-start(bf16[32,1024]{1,0:T(8,128)(2,1)S(1)} %get-tuple-element.11.src_ref), channel_id=1, source_target_pairs={{0,1},{1,0},{2,3},{3,2},{4,5},{5,4},{6,7},{7,6},{8,9},{9,8},{10,11... | collective-permute-start | bytes 196616 | tf_op jit(solution)/shard_map/ppermute | solution.py:231

commit v3 on v2

--- a/solution.py
+++ b/solution.py
@@ -88,10 +88,10 @@
         wanted = jnp.broadcast_to(ids, (elems, width))
         pick = jnp.where(wanted == lax.broadcasted_iota(jnp.int32, (elems, width), 0), 1.0, 0.0).astype(jnp.bfloat16)
         for pair in range(pairs):
-            if tile == 0 and pair % (pairs // 2) == 0:
-                copies[pair // (pairs // 2)].wait()
+            if tile == 0 and pair == 0:
+                [copy.wait() for copy in copies]
                 if shuffled:
-                    for p in range(pair, pair + pairs // 2):
+                    for p in range(pairs):
                         wide_ref[p] = chunk_ref[2 * rows * p : 2 * rows * p + 8 * shuffled, :].astype(jnp.float32)
             found = jnp.dot(
                 chunk_ref[2 * rows * pair + 8 * shuffled : 2 * rows * (pair + 1), :], pick, preferred_element_type=jnp.float32)
@@ -149,40 +149,33 @@
         before = before + part[:, LANES:]
 
 
-def place_own(n_panel, src_ref, owner_ref, pos_ref, weight_ref, out_ref, sorted_ref, wide_ref):
-    points = src_ref.shape[1]
+def place_own(n_panel, src_ref, owner_ref, pos_ref, out_ref):
+    rows, points = src_ref.shape
     size = owner_ref.shape[1] // n_panel
+    at = pl.ds(pl.multiple_of(lax.axis_index("obs") * points, points), points)
+    part = place(owner_ref[0:1, at], pos_ref[0:1, at], src_ref[...], n_panel, size).astype(jnp.bfloat16)
+    for p in range(n_panel):
+        out_ref[p] = part[p // 2 * rows : (p // 2 + 1) * rows, p % 2 * size : (p % 2 + 1) * size]
+
+
+def sort_weights(got_ref, weight_ref, offset_ref, sorted_ref, delay_ref, wide_ref):
     band, observers, width = sorted_ref.shape
+    size = weight_ref.shape[1]
     quants = width // size
+    delay_ref[...] = jnp.full(delay_ref.shape, offset_ref[0, 0].astype(jnp.float32))
     wide_ref[...] = weight_ref[...].astype(jnp.float32)
     for k in range(band):
         for q in range(quants):
             lane = pl.ds(k * quants + q, observers, stride=band * quants)
             sorted_ref[k, :, q * size : (q + 1) * size] = wide_ref[lane, :].astype(jnp.bfloat16)
-    at = pl.ds(pl.multiple_of(lax.axis_index("obs") * points, points), points)
-    out_ref[...] = place(owner_ref[0:1, at], pos_ref[0:1, at], src_ref[...], n_panel, size).astype(jnp.bfloat16)
-
-
-def place_rest(n_panel, n_obs, part_ref, owner_ref, pos_ref, offset_ref, *refs):
-    others, (out_ref, delay_ref) = refs[:-2], refs[-2:]
-    rows, points = others[0].shape
-    size = owner_ref.shape[1] // n_panel
-    delay_ref[...] = jnp.full(delay_ref.shape, offset_ref[0, 0].astype(jnp.float32))
-    total = part_ref[...].astype(jnp.float32)
-    for step in range(1, n_obs):
-        block = lax.rem(lax.axis_index("obs") + (n_obs - step), n_obs)
-        at = pl.ds(pl.multiple_of(block * points, points), points)
-        total = total + place(owner_ref[0:1, at], pos_ref[0:1, at], others[step - 1][...], n_panel, size)
-    total = total.astype(jnp.bfloat16)
-    for p in range(n_panel):
-        out_ref[p] = total[p // 2 * rows : (p // 2 + 1) * rows, p % 2 * size : (p % 2 + 1) * size]
-
-
-def band_sum(quants, band, got_ref, weight_ref, delay_ref, out_ref, lag_ref, shift_ref):
-    parts, rows, size = got_ref.shape
+
+
+def band_sum(quants, band, weight_ref, delay_ref, *refs):
+    got_refs, (out_ref, lag_ref, shift_ref) = refs[:-3], refs[-3:]
+    parts, rows, size = got_refs[0].shape
     times = rows // quants
     span = parts * times
-    values = got_ref[...].astype(jnp.float32)
+    values = sum(ref[...].astype(jnp.float32) for ref in got_refs)
     flat = jnp.concatenate(
         [values[:, q * times : (q + 1) * times, :].reshape(span, size).astype(jnp.bfloat16) for q in range(quants)],
         axis=1,
@@ -227,40 +220,39 @@
         ],
         name="interpolate",
     )(donor.reshape(times * nodes * quants, elems), donor_elem.reshape(1, points), local_coords, owner_row)
-    others = [
-        lax.ppermute(sources, "obs", [(s, (s + step) % n_obs) for s in range(n_obs)]) for step in range(1, n_obs)
-    ]
-    part, weight_rows = pl.pallas_call(
+    outgoing = pl.pallas_call(
         functools.partial(place_own, n_panel),
+        out_shape=pltpu.VMEM((n_panel, rows, size), jnp.bfloat16),
+        in_specs=[VM, VM, VM],
+        out_specs=VM,
+        name="place_own",
+    )(near(sources), near(owner_row), near(pos))
+    got = lax.all_to_all(outgoing, "panel", split_axis=0, concat_axis=0, tiled=True)
+    others = [lax.ppermute(got, "obs", [(s, (s + step) % n_obs) for s in range(n_obs)]) for step in range(1, n_obs)]
+    got, offsets = lax.optimization_barrier((got, offsets))
+    weight_rows, delay = pl.pallas_call(
+        sort_weights,
         out_shape=(
-            pltpu.VMEM((n_panel // 2 * rows, 2 * size), jnp.bfloat16),
             pltpu.VMEM((band, observers, quants * size), jnp.bfloat16),
+            pltpu.VMEM((1, LANES), jnp.float32),
         ),
-        in_specs=[VM, VM, VM, VM],
+        in_specs=[VM, VM, SM],
         out_specs=(VM, VM),
         scratch_shapes=[pltpu.VMEM((observers * band * quants, size), jnp.float32)],
-        name="place_own",
-    )(near(sources), near(owner_row), near(pos), near(weights.reshape(observers * band * quants, size)))
-    outgoing, delay = pl.pallas_call(
-        functools.partial(place_rest, n_panel, n_obs),
-        out_shape=(pltpu.VMEM((n_panel, rows, size), jnp.bfloat16), pltpu.VMEM((1, LANES), jnp.float32)),
-        in_specs=[VM, VM, VM, SM] + [VM] * (n_obs - 1),
-        out_specs=(VM, VM),
-        name="place_rest",
-    )(near(part), near(owner_row), near(pos), offsets, *[near(x) for x in others])
-    got = lax.all_to_all(outgoing, "panel", split_axis=0, concat_axis=0, tiled=True)
+        name="sort_weights",
+    )(near(got), near(weights.reshape(observers * band * quants, size)), offsets)
     span = n_panel * times
     partial = pl.pallas_call(
         functools.partial(band_sum, quants, band),
         out_shape=pltpu.VMEM((n_panel, times, observers), jnp.float32),
-        in_specs=[VM, VM, VM],
+        in_specs=[VM] * (2 + n_obs),
         out_specs=VM,
         scratch_shapes=[
             pltpu.VMEM((band - 1, 8 + span, observers), jnp.float32),
             pltpu.VMEM((2 * span, observers), jnp.float32),
         ],
         name="band_sum",
-    )(near(got), near(weight_rows), near(delay))
+    )(near(weight_rows), near(delay), near(got), *[near(x) if n_obs == 2 else x for x in others])
     shares = lax.all_to_all(partial, "panel", split_axis=0, concat_axis=0, tiled=True)
     return jnp.sum(shares, axis=0)
 

time: 33 us -> 32.1 us (0.973)
  starting transfers between devices: 0.54 us -> 0.01 us
  Pallas kernels: 4.66 us -> 4.25 us
    ppermute x1, starting transfers between devices: 0.54 us -> 0.01 us  [body(): lax.ppermute(got, 'obs', [(s, (s + step) % n_obs) for s in range(n_obs)])]
    pallas_call x2, Pallas kernels: 1.15 us -> 0.8 us  [the longest x1 0.42 us: body(): pl.pallas_call(sort_weights, out_shape=(pltpu.VMEM((band, observers, quan...]
    all_to_all x1, blocking collectives: 10.5 us -> 10.2 us  [body(): lax.all_to_all(partial, 'panel', split_axis=0, concat_axis=0, tiled=True)]
  transfers between devices with their start and end apart: 1 -> 1, of which waited for: 0 -> 1; matrix products, arithmetic and copies ran while one was open for 0% -> 0% of each run, Pallas kernels for 2% -> 1%
where the time goes in v3:
time: 32.1 us; the launch traced here: 31.9 us
  blocking collectives  26.1 us (81%)
  Pallas kernels  4.25 us (13%)
  between operations  0.7 us (2%)
  other arithmetic  0.61 us (2%)
    all_to_all x1, blocking collectives, body(): lax.all_to_all(outgoing, 'panel', split_axis=0, concat_axis=0, tiled=True)  15.9 us
    all_to_all x1, blocking collectives, body(): lax.all_to_all(partial, 'panel', split_axis=0, concat_axis=0, tiled=True)  10.2 us
    pallas_call x1, Pallas kernels, body(): pl.pallas_call(functools.partial(interpolate, donor.shape, SHUFFLED, n_pa...  3.13 us
  transfers between devices with their start and end apart: 1, of which 1 were waited for; matrix products, arithmetic and copies ran while one was open for 0% of the time, Pallas kernels for 1%

profile of v3, /device:TPU:0, one launch (start us, length us, event | category | flops | bytes accessed | tf_op | source)
XLA Modules:
  0.0 31.9 jit_solution(16100064593627982340)
XLA Ops:
  0.0 0.0 copy-start.1
  0.0 0.0 copy-start
  0.0 3.1 %interpolate.1 = (bf16[32,1024]{1,0:T(8,128)(2,1)S(1)}, s32[1,2048]{1,0:T(1,128)S(1)}) custom-call(bf16[4000,128]{1,0:T(8,128)(2,1)} %bitcast.7, s32[1,1024]{1,0:T(1,128)} %bitcast.8, f32[3,1024]{1,0:T(4,128)} %coords_src.1, s32[1,2048]{1,0:T(1,128)} %bitcast.5), custom_call_target="tpu_custom_call" | custom-call | tf_op jit(solution)/shard_map/interpolate/pallas_call | solution.py:206
  3.1 0.0 copy-done.1
  3.2 0.4 %place_own.1 = bf16[16,32,128]{2,1,0:T(8,128)(2,1)S(1)} custom-call(bf16[32,1024]{1,0:T(8,128)(2,1)S(1)} %get-tuple-element.11.src_ref, s32[1,2048]{1,0:T(1,128)S(1)} %bitcast.6, s32[1,2048]{1,0:T(1,128)S(1)} %get-tuple-element.12.pos_ref), custom_call_target="tpu_custom_call" | custom-call | tf_op jit(solution)/shard_map/place_own/pallas_call | solution.py:223
  3.5 15.9 %all_to_all.10.got_ref.refs_0_ = bf16[16,32,128]{2,1,0:T(8,128)(2,1)S(1)} all-to-all(bf16[16,32,128]{2,1,0:T(8,128)(2,1)S(1)} %place_own.1), channel_id=1, replica_groups=mesh['panel'=16,'obs'=2] {'panel'}, dimensions={0} | all-to-all | bytes 262144 | tf_op jit(solution)/shard_map/all_to_all | solution.py:230
  19.5 0.0 collective-permute-start
  20.1 0.0 copy-done
  20.1 0.4 %sort_weights.1 = (bf16[4,128,512]{2,1,0:T(8,128)(2,1)S(1)}, f32[1,128]{1,0:T(1,128)S(1)}) custom-call(bf16[16,32,128]{2,1,0:T(8,128)(2,1)S(1)} %all_to_all.10.got_ref.refs_0_, bf16[2048,128]{1,0:T(8,128)(2,1)S(1)} %bitcast.4, s32[1,1]{1,0:T(1,128)S(6)} %copy.7.offset_ref), custom_call_target="tpu_custom_call" | custom-call | tf_op jit(solution)/shard_map/sort_weights/pallas_call | solution.py:233
  20.6 0.3 collective-permute-done.refs_1_
  20.8 0.3 %band_sum.1 = f32[16,8,128]{2,1,0:T(8,128)S(1)} custom-call(bf16[4,128,512]{2,1,0:T(8,128)(2,1)S(1)} %get-tuple-element.15.weight_ref, f32[1,128]{1,0:T(1,128)S(1)} %get-tuple-element.16.delay_ref, bf16[16,32,128]{2,1,0:T(8,128)(2,1)S(1)} %all_to_all.10.got_ref.refs_0_, bf16[16,32,128]{2,1,0:T(8,128)(2,1)S(1)} %collective-permute-done.refs_1_), custom_call_target="tpu_custom_call" | custom-call | tf_op jit(solution)/shard_map/band_sum/pallas_call | solution.py:245
  21.2 10.2 %all_to_all.11 = f32[16,8,128]{2,1,0:T(8,128)S(1)} all-to-all(f32[16,8,128]{2,1,0:T(8,128)S(1)} %band_sum.1), channel_id=1, replica_groups=mesh['panel'=16,'obs'=2] {'panel'}, dimensions={0} | all-to-all | bytes 131072 | tf_op jit(solution)/shard_map/all_to_all | solution.py:256
  31.3 0.6 %reduce_sum.9 = f32[8,128]{1,0:T(8,128)} reduce(f32[16,8,128]{2,1,0:T(8,128)S(1)} %all_to_all.11, f32[]{:T(128)} %constant.0.clone.1), dimensions={0}, to_apply=%region_0.0 | reduce | flops 15360 | bytes 69636 | tf_op jit(solution)/shard_map/reduce_sum | solution.py:257
Async XLA Ops:
  0.0 3.1 %copy-start.1 = (s32[2048]{0:T(1024)S(1)}, s32[2048]{0:T(1024)}, u32[]{:S(2)}) copy-start(s32[2048]{0:T(1024)} %param.9) | copy-start | bytes 24580
  0.0 20.1 %copy-start = (bf16[128,4,4,128]{3,2,1,0:T(4,128)(2,1)S(1)}, bf16[128,4,4,128]{3,2,1,0:T(4,128)(2,1)}, u32[]{:S(2)}) copy-start(bf16[128,4,4,128]{3,2,1,0:T(4,128)(2,1)} %param.10) | copy-start | bytes 1572868
  19.5 1.3 %collective-permute-start = (bf16[16,32,128]{2,1,0:T(8,128)(2,1)S(1)}, bf16[16,32,128]{2,1,0:T(8,128)(2,1)S(1)}, u32[]{:S(2)}, u32[]{:S(2)}) collective-permute-start(bf16[16,32,128]{2,1,0:T(8,128)(2,1)S(1)} %all_to_all.10.got_ref.refs_0_), channel_id=1, source_target_pairs={{0,1},{1,0},{2,3},{3,2},{4,5},{5,4},{6,7},{7,6},{8,9},{9,8},{10,11... | collective-permute-start | bytes 393224 | tf_op jit(solution)/shard_map/ppermute | solution.py:231

commit v4 on v3

--- a/solution.py
+++ b/solution.py
@@ -172,10 +172,23 @@
 
 def band_sum(quants, band, weight_ref, delay_ref, *refs):
     got_refs, (out_ref, lag_ref, shift_ref) = refs[:-3], refs[-3:]
-    parts, rows, size = got_refs[0].shape
-    times = rows // quants
+    parts, times, observers = out_ref.shape
+    size = got_refs[0].shape[2]
     span = parts * times
-    values = sum(ref[...].astype(jnp.float32) for ref in got_refs)
+    held = [ref[...].astype(jnp.float32) for ref in got_refs]
+    if held[0].shape[0] == parts:
+        values = sum(held)
+    else:
+        n_obs = len(held)
+        held = [jnp.sum(x.reshape(parts, n_obs, x.shape[1], size), axis=1) for x in held]
+        me = lax.axis_index("obs")
+        chunks = []
+        for c in range(n_obs):
+            chunk = held[0]
+            for step in range(1, n_obs):
+                chunk = jnp.where(lax.rem(me + (n_obs - step), n_obs) == c, held[step], chunk)
+            chunks.append(chunk)
+        values = jnp.concatenate(chunks, axis=1)
     flat = jnp.concatenate(
         [values[:, q * times : (q + 1) * times, :].reshape(span, size).astype(jnp.bfloat16) for q in range(quants)],
         axis=1,
@@ -227,7 +240,11 @@
         out_specs=VM,
         name="place_own",
     )(near(sources), near(owner_row), near(pos))
-    got = lax.all_to_all(outgoing, "panel", split_axis=0, concat_axis=0, tiled=True)
+    if quants % n_obs == 0:
+        outgoing = outgoing.reshape(n_panel * n_obs, rows // n_obs, size)
+        got = lax.all_to_all(outgoing, ("panel", "obs"), split_axis=0, concat_axis=0, tiled=True)
+    else:
+        got = lax.all_to_all(outgoing, "panel", split_axis=0, concat_axis=0, tiled=True)
     others = [lax.ppermute(got, "obs", [(s, (s + step) % n_obs) for s in range(n_obs)]) for step in range(1, n_obs)]
     got, offsets = lax.optimization_barrier((got, offsets))
     weight_rows, delay = pl.pallas_call(

time: 32.1 us -> 31.7 us (0.988)
  blocking collectives: 26.1 us -> 25.6 us
    all_to_all x1, blocking collectives: 15.9 us -> 15.3 us  [body(): lax.all_to_all(outgoing, ('panel', 'obs'), split_axis=0, concat_axis=0, t...]
  transfers between devices with their start and end apart: 1 -> 1, of which waited for: 1 -> 0; matrix products, arithmetic and copies ran while one was open for 0% -> 0% of each run, Pallas kernels for 1% -> 1%
where the time goes in v4:
time: 31.7 us; the launch traced here: 31.5 us
  blocking collectives  25.6 us (81%)
  Pallas kernels  4.26 us (13%)
  between operations  0.69 us (2%)
  other arithmetic  0.61 us (2%)
    all_to_all x1, blocking collectives, body(): lax.all_to_all(outgoing, ('panel', 'obs'), split_axis=0, concat_axis=0, t...  15.3 us
    all_to_all x1, blocking collectives, body(): lax.all_to_all(partial, 'panel', split_axis=0, concat_axis=0, tiled=True)  10.3 us
    pallas_call x1, Pallas kernels, body(): pl.pallas_call(functools.partial(interpolate, donor.shape, SHUFFLED, n_pa...  3.13 us
  transfers between devices with their start and end apart: 1, of which 0 were waited for; matrix products, arithmetic and copies ran while one was open for 0% of the time, Pallas kernels for 1%

profile of v4, /device:TPU:0, one launch (start us, length us, event | category | flops | bytes accessed | tf_op | source)
XLA Modules:
  0.0 31.5 jit_solution(8928563052329210114)
XLA Ops:
  0.0 0.0 copy-start.1
  0.0 0.0 copy-start
  0.0 3.1 %interpolate.1 = (bf16[32,1024]{1,0:T(8,128)(2,1)S(1)}, s32[1,2048]{1,0:T(1,128)S(1)}) custom-call(bf16[4000,128]{1,0:T(8,128)(2,1)} %bitcast.9, s32[1,1024]{1,0:T(1,128)} %bitcast.10, f32[3,1024]{1,0:T(4,128)} %coords_src.1, s32[1,2048]{1,0:T(1,128)} %bitcast.7), custom_call_target="tpu_custom_call" | custom-call | tf_op jit(solution)/shard_map/interpolate/pallas_call | solution.py:219
  3.1 0.0 copy-done.1
  3.2 0.4 %place_own.1 = bf16[16,32,128]{2,1,0:T(8,128)(2,1)S(1)} custom-call(bf16[32,1024]{1,0:T(8,128)(2,1)S(1)} %get-tuple-element.11.src_ref, s32[1,2048]{1,0:T(1,128)S(1)} %bitcast.8, s32[1,2048]{1,0:T(1,128)S(1)} %get-tuple-element.12.pos_ref), custom_call_target="tpu_custom_call" | custom-call | tf_op jit(solution)/shard_map/place_own/pallas_call | solution.py:236
  3.5 15.3 %all_to_all.10.got_ref.refs_0_ = bf16[32,16,128]{2,1,0:T(8,128)(2,1)S(1)} all-to-all(bf16[32,16,128]{2,1,0:T(8,128)(2,1)S(1)} %bitcast.6), channel_id=1, replica_groups=mesh['panel'=16,'obs'=2] {'panel','obs'}, dimensions={0} | all-to-all | bytes 262144 | tf_op jit(solution)/shard_map/all_to_all | solution.py:245
  18.9 0.2 collective-permute-start
  19.8 0.0 copy-done
  19.8 0.4 %sort_weights.1 = (bf16[4,128,512]{2,1,0:T(8,128)(2,1)S(1)}, f32[1,128]{1,0:T(1,128)S(1)}) custom-call(bf16[32,16,128]{2,1,0:T(8,128)(2,1)S(1)} %all_to_all.10.got_ref.refs_0_, bf16[2048,128]{1,0:T(8,128)(2,1)S(1)} %bitcast.5, s32[1,1]{1,0:T(1,128)S(6)} %copy.7.offset_ref), custom_call_target="tpu_custom_call" | custom-call | tf_op jit(solution)/shard_map/sort_weights/pallas_call | solution.py:250
  20.2 0.0 collective-permute-done.refs_1_
  20.2 0.3 %band_sum.1 = f32[16,8,128]{2,1,0:T(8,128)S(1)} custom-call(bf16[4,128,512]{2,1,0:T(8,128)(2,1)S(1)} %get-tuple-element.15.weight_ref, f32[1,128]{1,0:T(1,128)S(1)} %get-tuple-element.16.delay_ref, bf16[32,16,128]{2,1,0:T(8,128)(2,1)S(1)} %all_to_all.10.got_ref.refs_0_, bf16[32,16,128]{2,1,0:T(8,128)(2,1)S(1)} %collective-permute-done.refs_1_), custom_call_target="tpu_custom_call" | custom-call | tf_op jit(solution)/shard_map/band_sum/pallas_call | solution.py:262
  20.6 10.3 %all_to_all.11 = f32[16,8,128]{2,1,0:T(8,128)S(1)} all-to-all(f32[16,8,128]{2,1,0:T(8,128)S(1)} %band_sum.1), channel_id=1, replica_groups=mesh['panel'=16,'obs'=2] {'panel'}, dimensions={0} | all-to-all | bytes 131072 | tf_op jit(solution)/shard_map/all_to_all | solution.py:273
  30.9 0.6 %reduce_sum.9 = f32[8,128]{1,0:T(8,128)} reduce(f32[16,8,128]{2,1,0:T(8,128)S(1)} %all_to_all.11, f32[]{:T(128)} %constant.0.clone.1), dimensions={0}, to_apply=%region_0.0 | reduce | flops 15360 | bytes 69636 | tf_op jit(solution)/shard_map/reduce_sum | solution.py:274
Async XLA Ops:
  0.0 3.1 %copy-start.1 = (s32[2048]{0:T(1024)S(1)}, s32[2048]{0:T(1024)}, u32[]{:S(2)}) copy-start(s32[2048]{0:T(1024)} %param.9) | copy-start | bytes 24580
  0.0 19.7 %copy-start = (bf16[128,4,4,128]{3,2,1,0:T(4,128)(2,1)S(1)}, bf16[128,4,4,128]{3,2,1,0:T(4,128)(2,1)}, u32[]{:S(2)}) copy-start(bf16[128,4,4,128]{3,2,1,0:T(4,128)(2,1)} %param.10) | copy-start | bytes 1572868
  18.9 1.3 %collective-permute-start = (bf16[32,16,128]{2,1,0:T(8,128)(2,1)S(1)}, bf16[32,16,128]{2,1,0:T(8,128)(2,1)S(1)}, u32[]{:S(2)}, u32[]{:S(2)}) collective-permute-start(bf16[32,16,128]{2,1,0:T(8,128)(2,1)S(1)} %all_to_all.10.got_ref.refs_0_), channel_id=1, source_target_pairs={{0,1},{1,0},{2,3},{3,2},{4,5},{5,4},{6,7},{7,6},{8,9},{9,8},{10,11... | collective-permute-start | bytes 393224 | tf_op jit(solution)/shard_map/ppermute | solution.py:248

commit v5 on v4

--- a/solution.py
+++ b/solution.py
@@ -170,9 +170,10 @@
             sorted_ref[k, :, q * size : (q + 1) * size] = wide_ref[lane, :].astype(jnp.bfloat16)
 
 
-def band_sum(quants, band, weight_ref, delay_ref, *refs):
+def band_sum(n_panel, quants, band, weight_ref, delay_ref, *refs):
     got_refs, (out_ref, lag_ref, shift_ref) = refs[:-3], refs[-3:]
-    parts, times, observers = out_ref.shape
+    times, observers = out_ref.shape[1:]
+    parts = n_panel
     size = got_refs[0].shape[2]
     span = parts * times
     held = [ref[...].astype(jnp.float32) for ref in got_refs]
@@ -203,7 +204,16 @@
         total = one if total is None else total + one
     shift_ref[0:span, :] = jnp.zeros_like(total)
     shift_ref[span : 2 * span, :] = total
-    out_ref[...] = shift_ref[pl.ds(span - jnp.max(delay_ref[...]).astype(jnp.int32), span), :].reshape(out_ref.shape)
+    moved = shift_ref[pl.ds(span - jnp.max(delay_ref[...]).astype(jnp.int32), span), :].reshape(parts, times, observers)
+    slots = out_ref.shape[0] // parts
+    if slots == 1:
+        out_ref[...] = moved
+    else:
+        me = lax.axis_index("obs")
+        for c in range(slots):
+            mine = jnp.where(me == c, moved, 0.0).astype(out_ref.dtype)
+            for p in range(parts):
+                out_ref[p * slots + c] = mine[p]
 
 
 def body(donor, donor_elem, local_coords, owner, weights, offsets):
@@ -259,9 +269,10 @@
         name="sort_weights",
     )(near(got), near(weights.reshape(observers * band * quants, size)), offsets)
     span = n_panel * times
+    slots = n_obs if n_obs == 2 else 1
     partial = pl.pallas_call(
-        functools.partial(band_sum, quants, band),
-        out_shape=pltpu.VMEM((n_panel, times, observers), jnp.float32),
+        functools.partial(band_sum, n_panel, quants, band),
+        out_shape=pltpu.VMEM((n_panel * slots, times, observers), jnp.float32 if slots > 1 else jnp.float32),
         in_specs=[VM] * (2 + n_obs),
         out_specs=VM,
         scratch_shapes=[
@@ -270,8 +281,9 @@
         ],
         name="band_sum",
     )(near(weight_rows), near(delay), near(got), *[near(x) if n_obs == 2 else x for x in others])
-    shares = lax.all_to_all(partial, "panel", split_axis=0, concat_axis=0, tiled=True)
-    return jnp.sum(shares, axis=0)
+    axes = ("panel", "obs") if slots > 1 else "panel"
+    shares = lax.all_to_all(partial, axes, split_axis=0, concat_axis=0, tiled=True)
+    return jnp.sum(shares.astype(jnp.float32), axis=0)
 
 
 def solution(mesh):

time: 31.7 us -> 31.3 us (0.987)
    all_to_all x1, blocking collectives: 10.3 us -> 9.97 us  [body(): lax.all_to_all(partial, axes, split_axis=0, concat_axis=0, tiled=True)]
where the time goes in v5:
time: 31.3 us; the launch traced here: 31.2 us
  blocking collectives  25.3 us (81%)
  Pallas kernels  4.27 us (14%)
  between operations  0.69 us (2%)
  other arithmetic  0.63 us (2%)
    all_to_all x1, blocking collectives, body(): lax.all_to_all(outgoing, ('panel', 'obs'), split_axis=0, concat_axis=0, t...  15.3 us
    all_to_all x1, blocking collectives, body(): lax.all_to_all(partial, axes, split_axis=0, concat_axis=0, tiled=True)  9.97 us
    pallas_call x1, Pallas kernels, body(): pl.pallas_call(functools.partial(interpolate, donor.shape, SHUFFLED, n_pa...  3.13 us
    reduce_sum x1, other arithmetic, body(): return jnp.sum(shares.astype(jnp.float32), axis=0)  0.63 us
  transfers between devices with their start and end apart: 1, of which 0 were waited for; matrix products, arithmetic and copies ran while one was open for 0% of the time, Pallas kernels for 1%

profile of v5, /device:TPU:0, one launch (start us, length us, event | category | flops | bytes accessed | tf_op | source)
XLA Modules:
  0.0 31.2 jit_solution(11582323285448829380)
XLA Ops:
  0.0 0.0 copy-start.1
  0.0 0.0 copy-start
  0.0 3.1 %interpolate.1 = (bf16[32,1024]{1,0:T(8,128)(2,1)S(1)}, s32[1,2048]{1,0:T(1,128)S(1)}) custom-call(bf16[4000,128]{1,0:T(8,128)(2,1)} %bitcast.9, s32[1,1024]{1,0:T(1,128)} %bitcast.10, f32[3,1024]{1,0:T(4,128)} %coords_src.1, s32[1,2048]{1,0:T(1,128)} %bitcast.7), custom_call_target="tpu_custom_call" | custom-call | tf_op jit(solution)/shard_map/interpolate/pallas_call | solution.py:229
  3.1 0.0 copy-done.1
  3.2 0.4 %place_own.1 = bf16[16,32,128]{2,1,0:T(8,128)(2,1)S(1)} custom-call(bf16[32,1024]{1,0:T(8,128)(2,1)S(1)} %get-tuple-element.11.src_ref, s32[1,2048]{1,0:T(1,128)S(1)} %bitcast.8, s32[1,2048]{1,0:T(1,128)S(1)} %get-tuple-element.12.pos_ref), custom_call_target="tpu_custom_call" | custom-call | tf_op jit(solution)/shard_map/place_own/pallas_call | solution.py:246
  3.5 15.3 %all_to_all.10.got_ref.refs_0_ = bf16[32,16,128]{2,1,0:T(8,128)(2,1)S(1)} all-to-all(bf16[32,16,128]{2,1,0:T(8,128)(2,1)S(1)} %bitcast.6), channel_id=1, replica_groups=mesh['panel'=16,'obs'=2] {'panel','obs'}, dimensions={0} | all-to-all | bytes 262144 | tf_op jit(solution)/shard_map/all_to_all | solution.py:255
  18.9 0.2 collective-permute-start
  19.8 0.0 copy-done
  19.8 0.4 %sort_weights.1 = (bf16[4,128,512]{2,1,0:T(8,128)(2,1)S(1)}, f32[1,128]{1,0:T(1,128)S(1)}) custom-call(bf16[32,16,128]{2,1,0:T(8,128)(2,1)S(1)} %all_to_all.10.got_ref.refs_0_, bf16[2048,128]{1,0:T(8,128)(2,1)S(1)} %bitcast.5, s32[1,1]{1,0:T(1,128)S(6)} %copy.7.offset_ref), custom_call_target="tpu_custom_call" | custom-call | tf_op jit(solution)/shard_map/sort_weights/pallas_call | solution.py:260
  20.2 0.0 collective-permute-done.refs_1_
  20.2 0.3 %band_sum.1 = f32[32,8,128]{2,1,0:T(8,128)S(1)} custom-call(bf16[4,128,512]{2,1,0:T(8,128)(2,1)S(1)} %get-tuple-element.15.weight_ref, f32[1,128]{1,0:T(1,128)S(1)} %get-tuple-element.16.delay_ref, bf16[32,16,128]{2,1,0:T(8,128)(2,1)S(1)} %all_to_all.10.got_ref.refs_0_, bf16[32,16,128]{2,1,0:T(8,128)(2,1)S(1)} %collective-permute-done.refs_1_), custom_call_target="tpu_custom_call" | custom-call | tf_op jit(solution)/shard_map/band_sum/pallas_call | solution.py:273
  20.6 10.0 %all_to_all.11 = f32[32,8,128]{2,1,0:T(8,128)S(1)} all-to-all(f32[32,8,128]{2,1,0:T(8,128)S(1)} %band_sum.1), channel_id=1, replica_groups=mesh['panel'=16,'obs'=2] {'panel','obs'}, dimensions={0} | all-to-all | bytes 262144 | tf_op jit(solution)/shard_map/all_to_all | solution.py:285
  30.5 0.6 %reduce_sum.9 = f32[8,128]{1,0:T(8,128)} reduce(f32[32,8,128]{2,1,0:T(8,128)S(1)} %all_to_all.11, f32[]{:T(128)} %constant.0.clone.1), dimensions={0}, to_apply=%region_0.0 | reduce | flops 31744 | bytes 135172 | tf_op jit(solution)/shard_map/reduce_sum | solution.py:286
Async XLA Ops:
  0.0 3.1 %copy-start.1 = (s32[2048]{0:T(1024)S(1)}, s32[2048]{0:T(1024)}, u32[]{:S(2)}) copy-start(s32[2048]{0:T(1024)} %param.9) | copy-start | bytes 24580
  0.0 19.7 %copy-start = (bf16[128,4,4,128]{3,2,1,0:T(4,128)(2,1)S(1)}, bf16[128,4,4,128]{3,2,1,0:T(4,128)(2,1)}, u32[]{:S(2)}) copy-start(bf16[128,4,4,128]{3,2,1,0:T(4,128)(2,1)} %param.10) | copy-start | bytes 1572868
  18.9 1.3 %collective-permute-start = (bf16[32,16,128]{2,1,0:T(8,128)(2,1)S(1)}, bf16[32,16,128]{2,1,0:T(8,128)(2,1)S(1)}, u32[]{:S(2)}, u32[]{:S(2)}) collective-permute-start(bf16[32,16,128]{2,1,0:T(8,128)(2,1)S(1)} %all_to_all.10.got_ref.refs_0_), channel_id=1, source_target_pairs={{0,1},{1,0},{2,3},{3,2},{4,5},{5,4},{6,7},{7,6},{8,9},{9,8},{10,11... | collective-permute-start | bytes 393224 | tf_op jit(solution)/shard_map/ppermute | solution.py:258

commit v6 on v5

--- a/solution.py
+++ b/solution.py
@@ -33,7 +33,7 @@
     return rows
 
 
-def interpolate(shape, shuffled, n_panel, donor_src, elem_src, coords_src, owner_src, out_ref, pos_ref, chunk_ref, elem_ref, coords_ref, owner_ref, wide_ref, table_ref, hold_ref, sems):
+def interpolate(shape, shuffled, n_panel, donor_src, elem_src, coords_src, owner_src, weight_src, out_ref, pos_ref, weight_ref, chunk_ref, elem_ref, coords_ref, owner_ref, wide_ref, table_ref, hold_ref, sems):
     times, nodes, quants, elems = shape
     points = coords_ref.shape[1]
     width = 2 * LANES
@@ -49,6 +49,7 @@
     ]
     first = pltpu.make_async_copy(coords_src, coords_ref, sems.at[1])
     second = pltpu.make_async_copy(elem_src, elem_ref, sems.at[2])
+    fourth = pltpu.make_async_copy(weight_src, weight_ref, sems.at[5])
     third = pltpu.make_async_copy(owner_src, owner_ref, sems.at[3])
     first.start()
     second.start()
@@ -89,7 +90,9 @@
         pick = jnp.where(wanted == lax.broadcasted_iota(jnp.int32, (elems, width), 0), 1.0, 0.0).astype(jnp.bfloat16)
         for pair in range(pairs):
             if tile == 0 and pair == 0:
-                [copy.wait() for copy in copies]
+                for copy in copies:
+                    copy.wait()
+                fourth.start()
                 if shuffled:
                     for p in range(pairs):
                         wide_ref[p] = chunk_ref[2 * rows * p : 2 * rows * p + 8 * shuffled, :].astype(jnp.float32)
@@ -115,6 +118,7 @@
                     row = q * times + 2 * pair + odd
                     hold_ref[row : row + 1, lanes] = total[q : q + 1]
     out_ref[...] = hold_ref[...].astype(jnp.bfloat16)
+    fourth.wait()
 
 
 def place(owner_row, pos_row, src, n_panel, size):
@@ -226,11 +230,15 @@
     observers, band = weights.shape[:2]
     rows = times * quants
     owner_row = owner.reshape(1, every)
-    sources, pos = pl.pallas_call(
+    sources, pos, raw = pl.pallas_call(
         functools.partial(interpolate, donor.shape, SHUFFLED, n_panel),
-        out_shape=(pltpu.VMEM((rows, points), jnp.bfloat16), pltpu.VMEM((1, every), jnp.int32)),
-        in_specs=[pl.BlockSpec(memory_space=pl.ANY)] * 4,
-        out_specs=(VM, VM),
+        out_shape=(
+            pltpu.VMEM((rows, points), jnp.bfloat16),
+            pltpu.VMEM((1, every), jnp.int32),
+            pltpu.VMEM((observers * band * quants, size), jnp.bfloat16),
+        ),
+        in_specs=[pl.BlockSpec(memory_space=pl.ANY)] * 5,
+        out_specs=(VM, VM, VM),
         scratch_shapes=[
             pltpu.VMEM((times * nodes * quants, elems), jnp.bfloat16),
             pltpu.VMEM((1, points), jnp.int32),
@@ -239,10 +247,10 @@
             pltpu.VMEM((times // 2, 8 * max(SHUFFLED, 1), elems), jnp.float32),
             pltpu.VMEM((2, 8 * ((nodes * quants + 7) // 8), 2 * LANES), jnp.float32),
             pltpu.VMEM((rows, points), jnp.float32),
-            pltpu.SemaphoreType.DMA((5,)),
+            pltpu.SemaphoreType.DMA((6,)),
         ],
         name="interpolate",
-    )(donor.reshape(times * nodes * quants, elems), donor_elem.reshape(1, points), local_coords, owner_row)
+    )(donor.reshape(times * nodes * quants, elems), donor_elem.reshape(1, points), local_coords, owner_row, weights.reshape(observers * band * quants, size))
     outgoing = pl.pallas_call(
         functools.partial(place_own, n_panel),
         out_shape=pltpu.VMEM((n_panel, rows, size), jnp.bfloat16),
@@ -267,7 +275,7 @@
         out_specs=(VM, VM),
         scratch_shapes=[pltpu.VMEM((observers * band * quants, size), jnp.float32)],
         name="sort_weights",
-    )(near(got), near(weights.reshape(observers * band * quants, size)), offsets)
+    )(near(got), near(raw), offsets)
     span = n_panel * times
     slots = n_obs if n_obs == 2 else 1
     partial = pl.pallas_call(

time: 31.3 us -> 31.3 us (level)
  transfers between devices with their start and end apart: 1 -> 1, of which waited for: 0 -> 1; matrix products, arithmetic and copies ran while one was open for 0% -> 0% of each run, Pallas kernels for 1% -> 1%
where the time goes in v6:
time: 31.3 us; the launch traced here: 31.1 us
  blocking collectives  25.3 us (81%)
  Pallas kernels  4.24 us (14%)
  between operations  0.69 us (2%)
  other arithmetic  0.63 us (2%)
    all_to_all x1, blocking collectives, body(): lax.all_to_all(outgoing, ('panel', 'obs'), split_axis=0, concat_axis=0, t...  15.3 us
    all_to_all x1, blocking collectives, body(): lax.all_to_all(partial, axes, split_axis=0, concat_axis=0, tiled=True)  9.97 us
    pallas_call x1, Pallas kernels, body(): pl.pallas_call(functools.partial(interpolate, donor.shape, SHUFFLED, n_pa...  3.1 us
    reduce_sum x1, other arithmetic, body(): return jnp.sum(shares.astype(jnp.float32), axis=0)  0.63 us
  transfers between devices with their start and end apart: 1, of which 1 were waited for; matrix products, arithmetic and copies ran while one was open for 0% of the time, Pallas kernels for 1%

profile of v6, /device:TPU:0, one launch (start us, length us, event | category | flops | bytes accessed | tf_op | source)
XLA Modules:
  0.0 31.1 jit_solution(12723590192359167504)
XLA Ops:
  0.0 0.0 copy-start
  0.0 3.1 %interpolate.1 = (bf16[32,1024]{1,0:T(8,128)(2,1)S(1)}, s32[1,2048]{1,0:T(1,128)S(1)}, bf16[2048,128]{1,0:T(8,128)(2,1)S(1)}) custom-call(bf16[4000,128]{1,0:T(8,128)(2,1)} %bitcast.8, s32[1,1024]{1,0:T(1,128)} %bitcast.10, f32[3,1024]{1,0:T(4,128)} %coords_src.1, s32[1,2048]{1,0:T(1,128)} %bitcast.6, bf16[2048,128]{1,0:T(8,128)(2,1)} %bitcast.9), custom_call_target="tpu_custom_call" | custom-call | tf_op jit(solution)/shard_map/interpolate/pallas_call | solution.py:233
  3.1 0.0 copy-done
  3.1 0.4 %place_own.1 = bf16[16,32,128]{2,1,0:T(8,128)(2,1)S(1)} custom-call(bf16[32,1024]{1,0:T(8,128)(2,1)S(1)} %get-tuple-element.12.src_ref, s32[1,2048]{1,0:T(1,128)S(1)} %bitcast.7, s32[1,2048]{1,0:T(1,128)S(1)} %get-tuple-element.13.pos_ref), custom_call_target="tpu_custom_call" | custom-call | tf_op jit(solution)/shard_map/place_own/pallas_call | solution.py:254
  3.5 15.3 %all_to_all.10.got_ref.refs_0_ = bf16[32,16,128]{2,1,0:T(8,128)(2,1)S(1)} all-to-all(bf16[32,16,128]{2,1,0:T(8,128)(2,1)S(1)} %bitcast.5), channel_id=1, replica_groups=mesh['panel'=16,'obs'=2] {'panel','obs'}, dimensions={0} | all-to-all | bytes 262144 | tf_op jit(solution)/shard_map/all_to_all | solution.py:263
  18.8 0.2 collective-permute-start
  19.7 0.4 %sort_weights.1 = (bf16[4,128,512]{2,1,0:T(8,128)(2,1)S(1)}, f32[1,128]{1,0:T(1,128)S(1)}) custom-call(bf16[32,16,128]{2,1,0:T(8,128)(2,1)S(1)} %all_to_all.10.got_ref.refs_0_, bf16[2048,128]{1,0:T(8,128)(2,1)S(1)} %get-tuple-element.15.weight_ref, s32[1,1]{1,0:T(1,128)S(6)} %copy.7.offset_ref), custom_call_target="tpu_custom_call" | custom-call | tf_op jit(solution)/shard_map/sort_weights/pallas_call | solution.py:268
  20.1 0.1 collective-permute-done.refs_1_
  20.2 0.3 %band_sum.1 = f32[32,8,128]{2,1,0:T(8,128)S(1)} custom-call(bf16[4,128,512]{2,1,0:T(8,128)(2,1)S(1)} %get-tuple-element.17.weight_ref, f32[1,128]{1,0:T(1,128)S(1)} %get-tuple-element.18.delay_ref, bf16[32,16,128]{2,1,0:T(8,128)(2,1)S(1)} %all_to_all.10.got_ref.refs_0_, bf16[32,16,128]{2,1,0:T(8,128)(2,1)S(1)} %collective-permute-done.refs_1_), custom_call_target="tpu_custom_call" | custom-call | tf_op jit(solution)/shard_map/band_sum/pallas_call | solution.py:281
  20.5 10.0 %all_to_all.11 = f32[32,8,128]{2,1,0:T(8,128)S(1)} all-to-all(f32[32,8,128]{2,1,0:T(8,128)S(1)} %band_sum.1), channel_id=1, replica_groups=mesh['panel'=16,'obs'=2] {'panel','obs'}, dimensions={0} | all-to-all | bytes 262144 | tf_op jit(solution)/shard_map/all_to_all | solution.py:293
  30.5 0.6 %reduce_sum.9 = f32[8,128]{1,0:T(8,128)} reduce(f32[32,8,128]{2,1,0:T(8,128)S(1)} %all_to_all.11, f32[]{:T(128)} %constant.0.clone.1), dimensions={0}, to_apply=%region_0.0 | reduce | flops 31744 | bytes 135172 | tf_op jit(solution)/shard_map/reduce_sum | solution.py:294
Async XLA Ops:
  0.0 3.1 %copy-start = (s32[2048]{0:T(1024)S(1)}, s32[2048]{0:T(1024)}, u32[]{:S(2)}) copy-start(s32[2048]{0:T(1024)} %param.9) | copy-start | bytes 24580
  18.8 1.3 %collective-permute-start = (bf16[32,16,128]{2,1,0:T(8,128)(2,1)S(1)}, bf16[32,16,128]{2,1,0:T(8,128)(2,1)S(1)}, u32[]{:S(2)}, u32[]{:S(2)}) collective-permute-start(bf16[32,16,128]{2,1,0:T(8,128)(2,1)S(1)} %all_to_all.10.got_ref.refs_0_), channel_id=1, source_target_pairs={{0,1},{1,0},{2,3},{3,2},{4,5},{5,4},{6,7},{7,6},{8,9},{9,8},{10,11... | collective-permute-start | bytes 393224 | tf_op jit(solution)/shard_map/ppermute | solution.py:266
